TPU v7x, 32 devices: a whole 2x2x4 slice. The times are simulated.
32 devices in a mesh: fsdp: 16 (over z, x, core), tensor: 2 (over y).
Axes of the slice: x: 2, y: 2, z: 4, core: 2. Of those that a mesh axis runs over, the one named last changes fastest.
Arguments:
- tokens: bfloat16 [8192, 1024], P(('fsdp', 'tensor')), may hold values from -6 to 6
- segments: int32 [16, 512], P('fsdp'), may hold values from 0 to 3, never falling along the last dimension, each value on 1 to 256 neighbouring positions
- norm_gains: float32 [2, 1024], P(None, ('fsdp', 'tensor')), may hold values from 0.5 to 1.5
- row_biases: float32 [4, 1024], P(None, ('fsdp', 'tensor')), may hold values from -3 to 3
- attention_in: bfloat16 [1024, 3, 1024], P('fsdp', None, 'tensor'), may hold values from -0.1875 to 0.1875
- query_bias: bfloat16 [16, 64], P('tensor', 'fsdp'), may hold values from -3 to 3
- value_bias: bfloat16 [16, 64], P('tensor', 'fsdp'), may hold values from -1.1953125 to 1.1953125
- attention_out: bfloat16 [1024, 1024], P('tensor', 'fsdp'), may hold values from -0.75 to 0.75
- hidden_in: bfloat16 [1024, 4096], P('fsdp', 'tensor'), may hold values from -0.1875 to 0.1875
- hidden_bias: bfloat16 [16, 256], P('tensor', 'fsdp'), may hold values from -3 to 3
- hidden_out: bfloat16 [4096, 1024], P('tensor', 'fsdp'), may hold values from -0.09375 to 0.09375
- output_grad: bfloat16 [8192, 1024], P(('fsdp', 'tensor')), may hold values from -6 to 6
Outputs:
- output: bfloat16 [8192, 1024], P(('fsdp', 'tensor'))
- tokens_grad: bfloat16 [8192, 1024], P(('fsdp', 'tensor'))
- attention_in_grad: float32 [1024, 3, 1024], P('fsdp', None, 'tensor')
- attention_out_grad: float32 [1024, 1024], P('tensor', 'fsdp')
- hidden_in_grad: float32 [1024, 4096], P('fsdp', 'tensor')
- hidden_out_grad: float32 [4096, 1024], P('tensor', 'fsdp')
- query_bias_grad: float32 [16, 64], P('tensor', 'fsdp')
- value_bias_grad: float32 [16, 64], P('tensor', 'fsdp')
- hidden_bias_grad: float32 [16, 256], P('tensor', 'fsdp')
- norm_gains_grad: float32 [2, 1024], P(None, ('fsdp', 'tensor'))
- row_biases_grad: float32 [4, 1024], P(None, ('fsdp', 'tensor'))
Inputs may be any that keep to these rules, and one draw needn't show every extreme that they name: `segments`: along each sequence segment numbers never fall; each sequence holds documents of 1 to 256 tokens, one of exactly 256.
All inputs are finite; a program needn't handle non-finite values.
Results may differ from a plain program's by a relative error of at most 0.017.
Values may be sent and summed in bfloat16 or wider, within the bound.
No kernel may reach another device: no remote copies, remote signals or barrier semaphores. Data moves between devices by JAX's collectives and lax.ppermute only.
A program may use at most 128 MiB of HBM per device.

v0:
```python
import math

import jax
import jax.numpy as jnp
import numpy as np
from jax import lax
from jax.experimental import pallas as pl
from jax.experimental.pallas import tpu as pltpu
from jax.sharding import PartitionSpec as P

HD = 64
EPS = 1e-05
GELU_C = math.sqrt(2.0 / math.pi)
GELU_A = 0.044715
MASKED = -1e30
BF16 = jnp.bfloat16
F32 = jnp.float32
LANES = 128
VMEM_LIMIT = 48 * 1024 * 1024


def gelu_parts(pre_act):
    square = pre_act * pre_act
    tanh_part = jnp.tanh(GELU_C * pre_act * (1.0 + GELU_A * square))
    half = 0.5 * (1.0 + tanh_part)
    slope = half + 0.5 * pre_act * (1.0 - tanh_part * tanh_part) * GELU_C * (
        1.0 + 3.0 * GELU_A * square
    )
    return pre_act * half, slope


def normalize(row_data):
    row_mean = jnp.mean(row_data, axis=-1, keepdims=True)
    centered = row_data - row_mean
    variance = jnp.mean(centered * centered, axis=-1, keepdims=True)
    inverse = lax.rsqrt(variance + EPS)
    return centered * inverse, inverse


def normalize_back(grad_rows, normed, inverse, gain_row):
    scaled = grad_rows * gain_row
    return inverse * (
        scaled
        - jnp.mean(scaled, axis=-1, keepdims=True)
        - normed * jnp.mean(scaled * normed, axis=-1, keepdims=True)
    )


def tie(*values):
    return lax.optimization_barrier(values)


def assemble(table, pieces):
    m, n = pieces[0].shape
    count = len(pieces)

    def copy(places, *refs):
        for i in range(count):
            refs[count][pl.ds(pl.multiple_of(places[i] * m, m), m), :] = refs[i][...]

    return pl.pallas_call(
        copy,
        in_specs=[pl.BlockSpec(memory_space=pltpu.SMEM)]
        + [pl.BlockSpec(memory_space=pltpu.VMEM)] * count,
        out_shape=jax.ShapeDtypeStruct((count * m, n), pieces[0].dtype),
        compiler_params=pltpu.CompilerParams(vmem_limit_bytes=VMEM_LIMIT),
        name="assemble",
    )(table, *pieces)


def row_blocks(table, sums, at, m, given=None):
    count = len(sums)
    widths = [own.shape[1] for own in sums]

    def read(places, *refs):
        for j, entry in enumerate(at):
            rows = pl.ds(pl.multiple_of(places[entry] * m, m), m)
            start = 0
            for i in range(count):
                spot = (slice(j * m, (j + 1) * m), slice(start, start + widths[i]))
                value = refs[i][rows, :]
                if given is not None:
                    value = (value.astype(F32) + refs[count][spot].astype(F32)).astype(BF16)
                refs[-1][spot] = value
                start += widths[i]

    arrays = [*sums] if given is None else [*sums, given]
    return pl.pallas_call(
        read,
        in_specs=[pl.BlockSpec(memory_space=pltpu.SMEM)]
        + [pl.BlockSpec(memory_space=pltpu.VMEM)] * len(arrays),
        out_shape=jax.ShapeDtypeStruct((len(at) * m, sum(widths)), BF16),
        compiler_params=pltpu.CompilerParams(vmem_limit_bytes=VMEM_LIMIT),
        name="row_blocks",
    )(table, *arrays)


def ring_add(own, numbers, arrived):
    lanes = len(numbers)
    shape = arrived[0].shape

    def add(*refs):
        for j in range(lanes):
            total = refs[j][...].astype(F32) + refs[lanes + j][...].astype(F32)
            refs[2 * lanes + j][...] = total.astype(BF16)

    blocks = [pl.BlockSpec(shape, lambda i, k=k: (k, 0)) for k in numbers]
    whole = pl.BlockSpec(shape, lambda i: (0, 0))
    return pl.pallas_call(
        add,
        grid=(1,),
        in_specs=blocks + [whole] * lanes,
        out_specs=[whole] * lanes,
        out_shape=[jax.ShapeDtypeStruct(shape, BF16)] * lanes,
        name="ring_add",
    )(*[own] * lanes, *arrived)


def paired_products(lefts, rights):
    depth, rows = lefts[0].shape
    width = rights[0].shape[1]
    tile = min(width, 512)
    half = width // tile

    def multiply(left_a, left_b, right_a, right_b, target, turned):
        j = pl.program_id(0)

        @pl.when(j == 0)
        def _():
            turned[...] = left_a[...].T

        @pl.when(j == half)
        def _():
            turned[...] = left_b[...].T

        @pl.when(j < half)
        def _():
            target[...] = dot(turned[...], right_a[...], ((1,), (0,))).astype(BF16)

        @pl.when(j >= half)
        def _():
            target[...] = dot(turned[...], right_b[...], ((1,), (0,))).astype(BF16)

    whole = pl.BlockSpec((depth, rows), lambda j: (0, 0))
    return pl.pallas_call(
        multiply,
        grid=(2 * half,),
        in_specs=[
            whole,
            whole,
            pl.BlockSpec((depth, tile), lambda j: (0, jnp.minimum(j, half - 1))),
            pl.BlockSpec((depth, tile), lambda j: (0, jnp.maximum(j - half, 0))),
        ],
        out_specs=pl.BlockSpec((rows, tile), lambda j: (0, j)),
        out_shape=jax.ShapeDtypeStruct((rows, 2 * width), BF16),
        scratch_shapes=[pltpu.VMEM((rows, depth), BF16)],
        compiler_params=pltpu.CompilerParams(vmem_limit_bytes=VMEM_LIMIT),
        name="paired_products",
    )(*lefts, *rights)


def allowed_pairs(column, row):
    shape = (column.shape[0], row.shape[1])
    causal = lax.broadcasted_iota(jnp.int32, shape, 0) <= lax.broadcasted_iota(jnp.int32, shape, 1)
    return causal & (column == row)


def probabilities(query, key, allowed):
    scores = jnp.where(allowed, dot(key, query, ((1,), (1,))), MASKED)
    terms = jnp.exp(scores - jnp.max(scores, axis=0, keepdims=True))
    return terms * (1.0 / jnp.sum(terms, axis=0, keepdims=True))


def attend(query_rows, key_rows, value_rows, segments, score_scale):
    seq_count, seq_len = segments.shape
    width = query_rows.shape[1]
    step = min(width, 2 * HD)

    def forward(column, row, query, key, value, mixed):
        allowed = allowed_pairs(column[...], row[0])
        for h in range(step // HD):
            at = slice(h * HD, (h + 1) * HD)
            probs = probabilities(query[:, at] * BF16(score_scale), key[:, at], allowed)
            mixed[:, at] = dot(value[:, at], probs.astype(BF16), ((0,), (0,))).T.astype(BF16)

    rows = pl.BlockSpec((seq_len, step), lambda i, j: (i, j))
    return pl.pallas_call(
        forward,
        grid=(seq_count, width // step),
        in_specs=[
            pl.BlockSpec((seq_len, 1), lambda i, j: (i, 0)),
            pl.BlockSpec((1, 1, seq_len), lambda i, j: (i, 0, 0)),
            rows,
            rows,
            rows,
        ],
        out_specs=rows,
        out_shape=jax.ShapeDtypeStruct(query_rows.shape, BF16),
        compiler_params=pltpu.CompilerParams(vmem_limit_bytes=VMEM_LIMIT),
        name="attend",
    )(
        segments.reshape(-1, 1),
        segments.reshape(seq_count, 1, seq_len),
        query_rows,
        key_rows,
        value_rows,
    )


def attend_back(query_rows, key_rows, value_rows, g_mixed, segments, score_scale):
    seq_count, seq_len = segments.shape
    width = query_rows.shape[1]
    step = min(width, 2 * HD)

    def backward(column, row, query, key, value, grad, g_query, g_key, g_value, sum_q, sum_v):
        allowed = allowed_pairs(column[...], row[0])
        for h in range(step // HD):
            at = slice(h * HD, (h + 1) * HD)
            q, k, v, g = query[:, at] * BF16(score_scale), key[:, at], value[:, at], grad[:, at]
            probs = probabilities(q, k, allowed)
            g_probs = dot(v, g, ((1,), (1,)))
            inner = jnp.sum(probs * g_probs, axis=0, keepdims=True)
            g_scores = (probs * (g_probs - inner)).astype(BF16)
            gv = dot(probs.astype(BF16), g, ((1,), (0,)))
            gq = dot(k, g_scores, ((0,), (0,))).T * score_scale
            g_query[:, at] = gq.astype(BF16)
            g_key[:, at] = dot(g_scores, q, ((1,), (0,))).astype(BF16)
            g_value[:, at] = gv.astype(BF16)
            sum_q[0, :, at] = jnp.sum(gq, axis=0, keepdims=True)
            sum_v[0, :, at] = jnp.sum(gv, axis=0, keepdims=True)

    rows = pl.BlockSpec((seq_len, step), lambda i, j: (i, j))
    sums = pl.BlockSpec((1, 1, step), lambda i, j: (i, 0, j))
    wide = jax.ShapeDtypeStruct(query_rows.shape, BF16)
    total = jax.ShapeDtypeStruct((seq_count, 1, width), F32)
    return pl.pallas_call(
        backward,
        grid=(seq_count, width // step),
        in_specs=[
            pl.BlockSpec((seq_len, 1), lambda i, j: (i, 0)),
            pl.BlockSpec((1, 1, seq_len), lambda i, j: (i, 0, 0)),
            rows,
            rows,
            rows,
            rows,
        ],
        out_specs=[rows, rows, rows, sums, sums],
        out_shape=[wide, wide, wide, total, total],
        compiler_params=pltpu.CompilerParams(vmem_limit_bytes=VMEM_LIMIT),
        name="attend_back",
    )(
        segments.reshape(-1, 1),
        segments.reshape(seq_count, 1, seq_len),
        query_rows,
        key_rows,
        value_rows,
        g_mixed,
    )


def dot(left, right, dims):
    return lax.dot_general(left, right, (dims, ((), ())), preferred_element_type=F32)


def pieces_of(value):
    pieces = []
    for _ in range(3):
        piece = lax.reduce_precision(value, 8, 7)
        pieces.append(piece.astype(BF16))
        value = value - piece
    return pieces


class Ring:
    def __init__(self, n_fsdp):
        self.size = n_fsdp
        self.chips = n_fsdp // 2
        second = n_fsdp // 8
        first = self.chips // second
        cycle = [(a, 0) for a in range(first)]
        for a in reversed(range(first)):
            across = list(range(1, second))
            cycle += [(a, b) for b in (across if a % 2 else reversed(across))]
        self.cycle = [a * second + b for a, b in cycle]
        self.place = {chip: p for p, chip in enumerate(self.cycle)}
        rows = []
        for device in range(n_fsdp):
            chip, core = device // 2, device % 2
            back = [self.cycle[(self.place[chip] - k) % self.chips] for k in range(self.chips)]
            rows.append([2 * c + core for c in back] + [2 * c + 1 - core for c in back])
        self.tables = np.asarray(rows, np.int32)

    def table(self):
        return jnp.asarray(self.tables)[lax.axis_index("fsdp")]

    def hop(self, value, core=0, along=0):
        pairs = []
        for source in range(self.size):
            place = (self.place[source // 2] + along) % self.chips
            pairs.append((source, 2 * self.cycle[place] + (source + core) % 2))
        return lax.ppermute(value, "fsdp", pairs)


class Gather:
    def __init__(self, ring, block):
        self.ring = ring
        self.up, self.down = [block], [block]

    def step(self):
        if len(self.up) <= self.ring.chips // 2:
            self.up.append(self.ring.hop(self.up[-1], along=1))
        if len(self.down) <= (self.ring.chips - 1) // 2:
            self.down.append(self.ring.hop(self.down[-1], along=-1))

    def before(self, *values):
        values = tie(*values, self.up[-1], self.down[-1])[: len(values)]
        return values if len(values) > 1 else values[0]

    def whole(self, table):
        while len(self.up) <= self.ring.chips // 2:
            self.step()
        own = self.up + self.down[:0:-1]
        return assemble(table, own + [self.ring.hop(piece, core=1) for piece in own])


class Scatter:
    def __init__(self, ring, table, sums):
        self.ring = ring
        self.chips = ring.chips
        self.widths = [own.shape[1] for own in sums]
        self.m = sums[0].shape[0] // ring.size
        away = row_blocks(table, sums, range(self.chips, 2 * self.chips), self.m)
        arrived = ring.hop(away, core=1)
        self.own = row_blocks(table, sums, range(self.chips), self.m, arrived)
        self.up = self.down = None
        self.done = 0

    def step(self):
        numbers = [self.chips // 2 - self.done]
        if self.chips // 2 + 1 + self.done < self.chips:
            numbers.append(self.chips // 2 + 1 + self.done)
        if self.done:
            moved = ring_add(self.own, numbers, [self.up, self.down][: len(numbers)])
        else:
            moved = [self.own[k * self.m : (k + 1) * self.m] for k in numbers]
        self.up = self.ring.hop(moved[0], along=-1)
        if len(numbers) > 1:
            self.down = self.ring.hop(moved[1], along=1)
        self.done += 1

    def before(self, *values):
        values = tie(*values, self.up, self.down)[: len(values)]
        return values if len(values) > 1 else values[0]

    def totals(self):
        while self.done < self.chips // 2:
            self.step()
        total = self.own[: self.m].astype(F32) + self.up.astype(F32) + self.down.astype(F32)
        ends = np.cumsum(self.widths)
        return [total[:, end - n : end] for n, end in zip(self.widths, ends)]


class Pair:
    def __init__(self, n_tensor):
        self.size = n_tensor

    def swap(self, value):
        return lax.ppermute(value, "tensor", [(0, 1), (1, 0)])

    def spread(self, own):
        if self.size != 2:
            return lax.all_gather(own, "tensor", axis=0, tiled=True)
        other = self.swap(own)
        first = lax.axis_index("tensor") == 0
        return jnp.concatenate(
            [jnp.where(first, own, other), jnp.where(first, other, own)], axis=0
        )

    def total(self, partial_rows):
        rounded = partial_rows.astype(BF16)
        if self.size != 2:
            return lax.psum(rounded.astype(F32), "tensor")
        return rounded.astype(F32) + self.swap(rounded).astype(F32)

    def collect(self, partial_rows):
        rounded = partial_rows.astype(BF16)
        if self.size != 2:
            return lax.psum_scatter(rounded, "tensor", scatter_dimension=0, tiled=True).astype(F32)
        rows = rounded.shape[0] // 2
        index = lax.axis_index("tensor")
        away = lax.dynamic_slice_in_dim(rounded, (1 - index) * rows, rows, 0)
        stay = lax.dynamic_slice_in_dim(rounded, index * rows, rows, 0)
        return stay.astype(F32) + self.swap(away).astype(F32)

    def sum(self, terms):
        if self.size != 2:
            return lax.psum(terms, "tensor")
        return terms + self.swap(terms)

    def own(self, rows_all):
        rows = rows_all.shape[0] // self.size
        return lax.dynamic_slice_in_dim(rows_all, lax.axis_index("tensor") * rows, rows, 0)


def layer(n_fsdp, n_tensor):
    ring = Ring(n_fsdp)
    pair = Pair(n_tensor)

    def shards(
        tokens,
        segments,
        norm_gains,
        row_biases,
        attention_in,
        query_bias,
        value_bias,
        attention_out,
        hidden_in,
        hidden_bias,
        hidden_out,
        output_grad,
    ):
        m = attention_in.shape[0]
        model_width = m * n_fsdp
        local_width = attention_in.shape[2]
        heads = query_bias.shape[0]
        hidden_width = hidden_in.shape[1]
        score_scale = 1.0 / math.sqrt(HD)
        q_len, h_len = query_bias.size, hidden_bias.size

        table = ring.table()
        six = pair.spread(jnp.concatenate([norm_gains, row_biases], axis=0).T)
        head_flat = jnp.concatenate(
            [query_bias.reshape(q_len), value_bias.reshape(q_len), hidden_bias.reshape(h_len)]
        )
        head_count = -(-head_flat.size // m)
        head_flat = jnp.pad(head_flat, (0, head_count * m - head_flat.size))
        columns = jnp.concatenate(
            pieces_of(six) + [head_flat.reshape(head_count, m).T],
            axis=1,
        )
        columns = jnp.pad(columns, ((0, 0), (0, LANES - columns.shape[1])))
        one = Gather(
            ring,
            jnp.concatenate(
                [attention_in.reshape(m, 3 * local_width), attention_out.T, columns], axis=1
            ),
        )
        one.step()
        hidden_block = jnp.concatenate([hidden_in, hidden_out.T], axis=1)
        hidden_block = one.before(hidden_block)
        hidden_full = lax.all_gather(hidden_block, "fsdp", axis=0, tiled=True)
        up_full, down_t = hidden_full[:, :hidden_width], hidden_full[:, hidden_width:]
        one.step()
        tok_rows = pair.spread(one.before(tokens)).astype(F32)
        one.step()
        grad_all = pair.spread(one.before(output_grad))
        normed_one, inverse_one = normalize(tok_rows)
        one_full = one.whole(table)
        in_full = one_full[:, : 3 * local_width]
        out_t = one_full[:, 3 * local_width : 4 * local_width]
        columns = one_full[:, 4 * local_width :]
        lanes = np.arange(LANES)[None, :]
        is_six = (lanes < 18) & (lanes % 6 == np.arange(6)[:, None])
        is_head = lanes == 18 + np.arange(head_count)[:, None]
        picked = np.concatenate([is_six, is_head], axis=0)
        picked = dot(jnp.asarray(picked, BF16), columns, ((1,), (1,)))
        gains_all, biases_all = picked[:2], picked[2:6]
        head_small = picked[6:].reshape(head_count, n_fsdp, m).transpose(1, 0, 2)
        head_small = head_small.reshape(n_fsdp, head_count * m)

        def head_row(start, length, width):
            return (
                head_small[:, start : start + length]
                .reshape(n_fsdp, heads, length // heads)
                .transpose(1, 0, 2)
                .reshape(width)
            )

        query_add = head_row(0, q_len, local_width)
        value_add = head_row(q_len, q_len, local_width)
        hidden_add = head_row(2 * q_len, h_len, hidden_width)

        in_one = (normed_one * gains_all[0] + biases_all[0]).astype(BF16)
        projected = dot(in_one, in_full, ((1,), (0,)))
        query_rows = (projected[:, :local_width] + query_add).astype(BF16)
        key_rows = projected[:, local_width : 2 * local_width].astype(BF16)
        value_rows = (projected[:, 2 * local_width :] + value_add).astype(BF16)
        query_rows, grad_all = tie(query_rows, grad_all)
        mixed_rows = attend(query_rows, key_rows, value_rows, segments, score_scale)
        attn_rows = pair.total(dot(mixed_rows, out_t, ((1,), (1,))))
        resid_rows = tok_rows + attn_rows + biases_all[1]
        normed_two, inverse_two = normalize(resid_rows)
        in_two = (normed_two * gains_all[1] + biases_all[2]).astype(BF16)
        pre_act = dot(in_two, up_full, ((1,), (0,))) + hidden_add
        act, slope = gelu_parts(pre_act)
        act_rows = act.astype(BF16)

        g_pre = dot(grad_all, down_t, ((1,), (0,))) * slope
        g_hidden_add = jnp.sum(g_pre, axis=0)
        g_pre_b = g_pre.astype(BF16)
        g_hidden = paired_products([grad_all, in_two], [act_rows, g_pre_b])
        g_pre_b, act_rows, g_hidden = tie(g_pre_b, act_rows, g_hidden)
        g_two_part = dot(g_pre_b, up_full, ((1,), (1,)))
        g_norm_two = pair.total(g_two_part)
        g_hidden_own = lax.psum_scatter(g_hidden, "fsdp", scatter_dimension=0, tiled=True)
        g_down_t, g_up = g_hidden_own[:, :hidden_width], g_hidden_own[:, hidden_width:]
        mlp_part = dot(act_rows, down_t, ((1,), (1,)))
        g_norm_two, mlp_part = tie(g_norm_two, mlp_part.astype(BF16))
        mlp_rows = pair.collect(mlp_part)
        result = (pair.own(resid_rows) + mlp_rows + biases_all[3]).astype(BF16)

        grad_rows = grad_all.astype(F32)
        g_resid = grad_rows + normalize_back(g_norm_two, normed_two, inverse_two, gains_all[1])
        g_resid_b = g_resid.astype(BF16)
        g_mixed = dot(g_resid_b, out_t, ((1,), (0,))).astype(BF16)
        g_query, g_keys, g_values, g_query_add, g_value_add = attend_back(
            query_rows, key_rows, value_rows, g_mixed, segments, score_scale
        )
        g_query_add = jnp.sum(g_query_add, axis=0)
        g_value_add = jnp.sum(g_value_add, axis=0)
        g_proj = jnp.concatenate([g_query, g_keys, g_values], axis=1)
        g_one_part = dot(g_proj, in_full, ((1,), (1,)))

        six_terms = jnp.stack(
            [
                jnp.sum(g_one_part * normed_one, axis=0),
                jnp.sum(g_two_part * normed_two, axis=0),
                jnp.sum(g_one_part, axis=0),
                jnp.sum(pair.own(g_resid), axis=0),
                jnp.sum(g_two_part, axis=0),
                jnp.sum(pair.own(grad_rows), axis=0),
            ]
        )
        six_terms = pair.sum(six_terms)

        def head_blocks(row, length):
            return (
                row.reshape(heads, n_fsdp, length // heads)
                .transpose(1, 0, 2)
                .reshape(n_fsdp, length)
            )

        head_terms = jnp.concatenate(
            [
                head_blocks(g_query_add, q_len),
                head_blocks(g_value_add, q_len),
                head_blocks(g_hidden_add, h_len),
            ],
            axis=1,
        )
        head_terms = jnp.pad(head_terms, ((0, 0), (0, head_count * m - head_terms.shape[1])))
        head_terms = head_terms.reshape(n_fsdp, head_count, m).transpose(1, 0, 2)
        head_terms = head_terms.reshape(head_count, model_width)
        small = jnp.concatenate([six_terms, head_terms], axis=0).astype(BF16)
        spots = jnp.asarray(np.arange(6 + head_count)[:, None] == lanes, BF16)
        small = dot(small, spots, ((0,), (0,))).astype(BF16)

        outer = Scatter(
            ring,
            table,
            [
                dot(in_one, g_proj, ((0,), (0,))).astype(BF16),
                dot(g_resid_b, mixed_rows, ((0,), (0,))).astype(BF16),
                small,
            ],
        )
        outer.step()
        g_one_part = outer.before(g_one_part.astype(BF16))
        g_norm_one = pair.collect(g_one_part)
        outer.step()
        tokens_grad = (
            pair.own(g_resid)
            + normalize_back(g_norm_one, pair.own(normed_one), pair.own(inverse_one), gains_all[0])
        ).astype(BF16)
        g_in, g_out_t, small = outer.totals()
        small = small.T
        six_sum = lax.dynamic_slice_in_dim(
            small[:6], lax.axis_index("tensor") * (m // n_tensor), m // n_tensor, 1
        )
        head_sum = small[6 : 6 + head_count].reshape(head_count * m)
        return (
            result,
            tokens_grad,
            g_in.reshape(m, 3, local_width),
            g_out_t.T,
            g_up.astype(F32),
            g_down_t.T.astype(F32),
            head_sum[:q_len].reshape(query_bias.shape),
            head_sum[q_len : 2 * q_len].reshape(value_bias.shape),
            head_sum[2 * q_len : 2 * q_len + h_len].reshape(hidden_bias.shape),
            six_sum[:2],
            six_sum[2:],
        )

    return shards


def solution(mesh):
    n_fsdp = mesh.shape["fsdp"]
    n_tensor = mesh.shape["tensor"]
    rows = P(("fsdp", "tensor"), None)
    columns = P(None, ("fsdp", "tensor"))
    head = P("tensor", "fsdp")
    into = P("fsdp", None, "tensor")
    up = P("fsdp", "tensor")
    return jax.shard_map(
        layer(n_fsdp, n_tensor),
        mesh=mesh,
        in_specs=(
            rows,
            P("fsdp", None),
            columns,
            columns,
            into,
            head,
            head,
            head,
            up,
            head,
            head,
            rows,
        ),
        out_specs=(rows, rows, into, head, up, head, head, head, head, columns, columns),
        check_vma=False,
    )
```

profile of v0, /device:TPU:0, one launch (start us, length us, event | category | flops | bytes accessed | tf_op | source)
XLA Modules:
  0.0 285.1 jit_solution(13847027832731851043)
XLA Ops:
  8.0 3.0 %collective-permute-start = (f32[32,6]{0,1:T(8,128)S(1)}, f32[32,6]{0,1:T(8,128)S(1)}, u32[]{:S(2)}, u32[]{:S(2)}) collective-permute-start(f32[32,6]{0,1:T(8,128)S(1)} %maximum_bitcast_fusion), channel_id=1, source_target_pairs={{0,1},{1,0},{2,3},{3,2},{4,5},{5,4},{6,7},{7,6},{8,9},{9,8},{10,11... | collective-permute-start | bytes 2312 | tf_op jit(solution)/shard_map/ppermute | solution.py:368
  20.3 4.2 %collective-permute-done.3.refs_7_ = bf16[64,2176]{1,0:T(8,128)(2,1)S(1)} collective-permute-done((bf16[64,2176]{1,0:T(8,128)(2,1)S(1)}, bf16[64,2176]{1,0:T(8,128)(2,1)S(1)}, u32[]{:S(2)}, u32[]{:S(2)}) %collective-permute-start.3) | collective-permute-done | bytes 278560 | tf_op jit(solution)/shard_map/ppermute | solution.py:301
  27.9 4.9 %collective-permute-done.4.refs_6_ = bf16[64,2176]{1,0:T(8,128)(2,1)S(1)} collective-permute-done((bf16[64,2176]{1,0:T(8,128)(2,1)S(1)}, bf16[64,2176]{1,0:T(8,128)(2,1)S(1)}, u32[]{:S(2)}, u32[]{:S(2)}) %collective-permute-start.4) | collective-permute-done | bytes 278560 | tf_op jit(solution)/shard_map/ppermute | solution.py:301
  38.0 15.1 %collective-permute-done.8.refs_5_ = bf16[64,2176]{1,0:T(8,128)(2,1)S(1)} collective-permute-done((bf16[64,2176]{1,0:T(8,128)(2,1)S(1)}, bf16[64,2176]{1,0:T(8,128)(2,1)S(1)}, u32[]{:S(2)}, u32[]{:S(2)}) %collective-permute-start.8) | collective-permute-done | bytes 278560 | tf_op jit(solution)/shard_map/ppermute | solution.py:301
  58.2 7.7 %collective-permute-done.7.refs_4_ = bf16[64,2176]{1,0:T(8,128)(2,1)S(1)} collective-permute-done((bf16[64,2176]{1,0:T(8,128)(2,1)S(1)}, bf16[64,2176]{1,0:T(8,128)(2,1)S(1)}, u32[]{:S(2)}, u32[]{:S(2)}) %collective-permute-start.7) | collective-permute-done | bytes 278560 | tf_op jit(solution)/shard_map/ppermute | solution.py:301
  69.2 2.9 %assemble.1 = bf16[1024,2176]{1,0:T(8,128)(2,1)} custom-call(s32[16]{0:T(128)S(1)} %fusion.35.places, bf16[64,2176]{1,0:T(8,128)(2,1)S(1)} %fusion.30.refs_0_, bf16[64,2176]{1,0:T(8,128)(2,1)S(1)} %collective-permute-done.1.refs_1_, bf16[64,2176]{1,0:T(8,128)(2,1)S(1)} %collective-permute-done.2.refs_2_, ...), custom_call_target="tpu_custom_call" | custom-call | tf_op jit(solution)/shard_map/assemble/pallas_call | solution.py:61
  74.8 4.1 %fusion.10 = f32[512,1536]{1,0:T(8,128)S(1)} fusion(bf16[1024,2176]{1,0:T(8,128)(2,1)} %assemble.1, f32[1024]{0:T(1024)S(1)} %bitcast.105, f32[1024]{0:T(1024)S(1)} %bitcast.90, f32[512]{0:T(512)S(1)} %add_rsqrt_fusion.1, f32[512]{0:T(512)S(1)} %broadcast_multiply_fusion.3, bf16[256,1024]{1,0:T(8,128)(2,1)} %copy-done.16, bf16[256,1024]{1,0:T(8,128)(2,1)} %copy-done.14), kind=kOutput, calls=%fused_computation.18 | convolution fusion | flops 1615331328 | bytes 7352320 | tf_op jit(solution)/shard_map/dot_general | solution.py:262
  79.3 5.7 %attend.1 = bf16[512,512]{1,0:T(8,128)(2,1)S(1)} custom-call(s32[512,1]{1,0:T(8,128)S(1)} %copy.97.column, s32[1,1,512]{2,1,0:T(1,128)S(1)} %bitcast.69, bf16[512,512]{1,0:T(8,128)(2,1)S(1)} %get-tuple-element.33.query, bf16[512,512]{1,0:T(8,128)(2,1)S(1)} %slice.217.key, bf16[512,512]{1,0:T(8,128)(2,1)S(1)} %get-tuple-element.107.value), custom_call_target="tpu_custom_call" | custom-call | tf_op jit(solution)/shard_map/attend/pallas_call | solution.py:187
  85.1 3.0 %convolution_convert_fusion.2 = bf16[512,1024]{1,0:T(8,128)(2,1)} fusion(bf16[512,512]{1,0:T(8,128)(2,1)S(1)} %attend.1, bf16[1024,2176]{1,0:T(8,128)(2,1)} %assemble.1), kind=kOutput, calls=%fused_computation.35 | convolution fusion | flops 537395200 | bytes 2621440 | tf_op jit(solution)/shard_map/dot_general | solution.py:262
  89.8 23.9 %collective-permute-done.18 = bf16[512,1024]{1,0:T(8,128)(2,1)} collective-permute-done((bf16[512,1024]{1,0:T(8,128)(2,1)}, bf16[512,1024]{1,0:T(8,128)(2,1)}, u32[]{:S(2)}, u32[]{:S(2)}) %collective-permute-start.18) | collective-permute-done | bytes 1048608 | tf_op jit(solution)/shard_map/ppermute | solution.py:368
  118.8 5.5 %multiply_convert_fusion = (bf16[512,2048]{1,0:T(8,128)(2,1)S(1)}, f32[512,2048]{1,0:T(8,128)S(1)}) fusion(f32[2048]{0:T(1024)S(1)} %add.181, bf16[512,1024]{1,0:T(8,128)(2,1)} %add_convert_fusion.left_b, bf16[1024,4096]{1,0:T(8,128)(2,1)} %all-gather.2.cloned.1.call-done), kind=kOutput, calls=%fused_computation | convolution fusion | flops 2157969408 | bytes 11542528 | tf_op jit(solution)/shard_map/dot_general | solution.py:262
  124.3 5.6 %fusion.41 = (bf16[2048]{0:T(1024)(128)(2,1)S(1)}, bf16[512,2048]{1,0:T(8,128)(2,1)}) fusion(f32[512,2048]{1,0:T(8,128)S(1)} %get-tuple-element.136, f32[2048]{0:T(1024)S(1)} %add.181, bf16[512,1024]{1,0:T(8,128)(2,1)S(1)} %pad_maximum_fusion.1.left_a, bf16[1024,4096]{1,0:T(8,128)(2,1)S(1)} %copy-done.38), kind=kOutput, calls=%fused_computation.110 | convolution fusion | flops 2168453120 | bytes 11546624 | tf_op jit(solution)/shard_map/dot_general | solution.py:262
  129.9 10.1 %paired_products.1 = bf16[1024,4096]{1,0:T(8,128)(2,1)} custom-call(bf16[512,1024]{1,0:T(8,128)(2,1)S(1)} %pad_maximum_fusion.1.left_a, bf16[512,1024]{1,0:T(8,128)(2,1)S(1)} %copy-done.1, bf16[512,2048]{1,0:T(8,128)(2,1)S(1)} %get-tuple-element.37.right_a, bf16[512,2048]{1,0:T(8,128)(2,1)} %get-tuple-element.36.right_b), custom_call_target="tpu_custom_call" | custom-call | tf_op jit(solution)/shard_map/paired_products/pallas_call | solution.py:145
  140.0 6.9 %fusion.46 = (bf16[512,1024]{1,0:T(8,128)(2,1)}, f32[512,1024]{1,0:T(8,128)}) fusion(bf16[512,2048]{1,0:T(8,128)(2,1)} %get-tuple-element.36.right_b, bf16[1024,4096]{1,0:T(8,128)(2,1)} %all-gather.2.cloned.1.call-done), kind=kOutput, calls=%fused_computation.115 | convolution fusion | flops 2148007936 | bytes 9437184 | tf_op jit(solution)/shard_map/dot_general | solution.py:262
  148.9 6.7 %fusion.18 = bf16[512,1024]{1,0:T(8,128)(2,1)} fusion(bf16[512,2048]{1,0:T(8,128)(2,1)} %copy-done.2, bf16[1024,4096]{1,0:T(8,128)(2,1)} %all-gather.2.cloned.1.call-done), kind=kOutput, calls=%fused_computation.36 | convolution fusion | flops 2148007936 | bytes 7340032 | tf_op jit(solution)/shard_map/dot_general | solution.py:262
  155.6 16.0 %collective-permute-done.19 = bf16[512,1024]{1,0:T(8,128)(2,1)} collective-permute-done((bf16[512,1024]{1,0:T(8,128)(2,1)}, bf16[512,1024]{1,0:T(8,128)(2,1)}, u32[]{:S(2)}, u32[]{:S(2)}) %collective-permute-start.19) | collective-permute-done | bytes 1048608 | tf_op jit(solution)/shard_map/ppermute | solution.py:368
  178.7 9.7 %attend_back.1 = (bf16[512,512]{1,0:T(8,128)(2,1)S(1)}, bf16[512,512]{1,0:T(8,128)(2,1)S(1)}, bf16[512,512]{1,0:T(8,128)(2,1)S(1)}, f32[1,1,512]{2,1,0:T(1,128)S(1)}, f32[1,1,512]{2,1,0:T(1,128)S(1)}) custom-call(s32[512,1]{1,0:T(8,128)S(1)} %copy.97.column, s32[1,1,512]{2,1,0:T(1,128)S(1)} %bitcast.70, bf16[512,512]{1,0:T(8,128)(2,1)S(1)} %get-tuple-element.33.query, ...), custom_call_target="tpu_custom_call" | custom-call | tf_op jit(solution)/shard_map/attend_back/pallas_call | solution.py:236
  194.5 6.1 %fusion.38 = (f32[1024]{0:T(1024)S(1)}, f32[1024]{0:T(1024)S(1)}, bf16[512,1024]{1,0:T(8,128)(2,1)}, f32[512,1024]{1,0:T(8,128)}) fusion(f32[512]{0:T(512)S(1)} %copy-done.32, f32[512]{0:T(512)S(1)} %copy-done.30, bf16[256,1024]{1,0:T(8,128)(2,1)S(1)} %copy-done.17, bf16[256,1024]{1,0:T(8,128)(2,1)S(1)} %copy-done.15, ...), kind=kOutput, calls=%fused_computation.108 | convolution fusion | flops 1615853568 | bytes 8925184 | tf_op jit(solution)/shard_map/dot_general | solution.py:262
  203.1 3.7 %convolution_convert_fusion.refs_0_ = bf16[1024,1536]{1,0:T(8,128)(2,1)} fusion(bf16[512,1536]{1,0:T(8,128)(2,1)S(1)} %copy-done.26, f32[1024]{0:T(1024)S(1)} %bitcast.106, f32[1024]{0:T(1024)S(1)} %bitcast.91, f32[512]{0:T(512)S(1)} %copy-done.32, f32[512]{0:T(512)S(1)} %copy-done.30, bf16[256,1024]{1,0:T(8,128)(2,1)S(1)} %copy-done.18, ...), kind=kOutput, calls=%fused_computation.4 | convolution fusion | flops 1616904192 | bytes 5779456 | tf_op jit(solution)/shard_map/dot_general | solution.py:262
  209.5 4.3 %collective-permute-done.22.refs_3_ = bf16[512,2176]{1,0:T(8,128)(2,1)S(1)} collective-permute-done((bf16[512,2176]{1,0:T(8,128)(2,1)S(1)}, bf16[512,2176]{1,0:T(8,128)(2,1)S(1)}, u32[]{:S(2)}, u32[]{:S(2)}) %collective-permute-start.22) | collective-permute-done | bytes 2228256 | tf_op jit(solution)/shard_map/ppermute | solution.py:301
  222.4 4.6 %collective-permute-done.24.refs_3_ = bf16[64,2176]{1,0:T(8,128)(2,1)} collective-permute-done((bf16[64,2176]{1,0:T(8,128)(2,1)}, bf16[64,2176]{1,0:T(8,128)(2,1)}, u32[]{:S(2)}, u32[]{:S(2)}) %collective-permute-start.24) | collective-permute-done | bytes 278560 | tf_op jit(solution)/shard_map/ppermute | solution.py:301
  238.8 10.1 %collective-permute-done.26.refs_2_ = bf16[64,2176]{1,0:T(8,128)(2,1)S(1)} collective-permute-done((bf16[64,2176]{1,0:T(8,128)(2,1)}, bf16[64,2176]{1,0:T(8,128)(2,1)S(1)}, u32[]{:S(2)}, u32[]{:S(2)}) %collective-permute-start.26) | collective-permute-done | bytes 278560 | tf_op jit(solution)/shard_map/ppermute | solution.py:301
  256.3 4.4 %collective-permute-done.28.refs_1_ = bf16[64,2176]{1,0:T(8,128)(2,1)} collective-permute-done((bf16[64,2176]{1,0:T(8,128)(2,1)}, bf16[64,2176]{1,0:T(8,128)(2,1)}, u32[]{:S(2)}, u32[]{:S(2)}) %collective-permute-start.28) | collective-permute-done | bytes 278560 | tf_op jit(solution)/shard_map/ppermute | solution.py:301
  266.2 3.6 %collective-permute-done.29 = bf16[64,2176]{1,0:T(8,128)(2,1)S(1)} collective-permute-done((bf16[64,2176]{1,0:T(8,128)(2,1)}, bf16[64,2176]{1,0:T(8,128)(2,1)S(1)}, u32[]{:S(2)}, u32[]{:S(2)}) %collective-permute-start.29) | collective-permute-done | bytes 278560 | tf_op jit(solution)/shard_map/ppermute | solution.py:301
  (245 shorter events, 98.5 us)
Async XLA Ops:
  7.2 111.6 %all-gather.2.cloned.1.call-start = ((), (), s32[]{:S(2)}) async-start(), calls=%async_computation.1 | async-start | bytes 8912896 | tf_op jit(solution)/shard_map/all_gather | solution.py:452
  16.4 8.2 %collective-permute-start.3 = (bf16[64,2176]{1,0:T(8,128)(2,1)S(1)}, bf16[64,2176]{1,0:T(8,128)(2,1)S(1)}, u32[]{:S(2)}, u32[]{:S(2)}) collective-permute-start(bf16[64,2176]{1,0:T(8,128)(2,1)S(1)} %fusion.30.refs_0_), channel_id=1, source_target_pairs={{0,4},{2,6},{4,12},{6,14},{8,0},{10,2},{12,20},{14,22},{16,8},{18,... | collective-permute-start | bytes 835592 | tf_op jit(solution)/shard_map/ppermute | solution.py:301
  17.9 7.8 %collective-permute-start.1 = (bf16[64,2176]{1,0:T(8,128)(2,1)S(1)}, bf16[64,2176]{1,0:T(8,128)(2,1)S(1)}, u32[]{:S(2)}, u32[]{:S(2)}) collective-permute-start(bf16[64,2176]{1,0:T(8,128)(2,1)S(1)} %fusion.30.refs_0_), channel_id=1, source_target_pairs={{0,8},{2,10},{4,0},{6,2},{8,16},{10,18},{12,4},{14,6},{16,24},{18,... | collective-permute-start | bytes 835592 | tf_op jit(solution)/shard_map/ppermute | solution.py:301
  25.8 250.4 %reduce-scatter.2.cloned.1.call-start = ((), (), s32[]{:S(2)}) async-start(), calls=%async_computation.2 | async-start | bytes 8912896 | tf_op jit(solution)/shard_map/reduce_scatter | solution.py:506
  34.1 20.6 %collective-permute-start.5 = (bf16[256,1024]{1,0:T(8,128)(2,1)S(1)}, bf16[256,1024]{1,0:T(8,128)(2,1)S(1)}, u32[]{:S(2)}, u32[]{:S(2)}) collective-permute-start(bf16[256,1024]{1,0:T(8,128)(2,1)S(1)} %copy-done.21), channel_id=1, source_target_pairs={{0,1},{1,0},{2,3},{3,2},{4,5},{5,4},{6,7},{7,6},{8,9},{9,8},{10,11... | collective-permute-start | bytes 1572872 | tf_op jit(solution)/shard_map/ppermute | solution.py:368
  34.6 18.5 %collective-permute-start.8 = (bf16[64,2176]{1,0:T(8,128)(2,1)S(1)}, bf16[64,2176]{1,0:T(8,128)(2,1)S(1)}, u32[]{:S(2)}, u32[]{:S(2)}) collective-permute-start(bf16[64,2176]{1,0:T(8,128)(2,1)S(1)} %collective-permute-done.4.refs_6_), channel_id=1, source_target_pairs={{0,4},{2,6},{4,12},{6,14},{8,0},{10,2},{12,20},{14,22},{16,8},{18,... | collective-permute-start | bytes 835592 | tf_op jit(solution)/shard_map/ppermute | solution.py:301
  36.2 17.0 %collective-permute-start.6 = (bf16[64,2176]{1,0:T(8,128)(2,1)S(1)}, bf16[64,2176]{1,0:T(8,128)(2,1)S(1)}, u32[]{:S(2)}, u32[]{:S(2)}) collective-permute-start(bf16[64,2176]{1,0:T(8,128)(2,1)S(1)} %collective-permute-done.2.refs_2_), channel_id=1, source_target_pairs={{0,8},{2,10},{4,0},{6,2},{8,16},{10,18},{12,4},{14,6},{16,24},{18,... | collective-permute-start | bytes 835592 | tf_op jit(solution)/shard_map/ppermute | solution.py:301
  37.5 19.9 %collective-permute-start.9 = (bf16[64,2176]{1,0:T(8,128)(2,1)S(1)}, bf16[64,2176]{1,0:T(8,128)(2,1)S(1)}, u32[]{:S(2)}, u32[]{:S(2)}) collective-permute-start(bf16[64,2176]{1,0:T(8,128)(2,1)S(1)} %fusion.30.refs_0_), channel_id=1, source_target_pairs={{0,2},{2,0},{4,6},{6,4},{8,10},{10,8},{12,14},{14,12},{16,18},{18,... | collective-permute-start | bytes 835592 | tf_op jit(solution)/shard_map/ppermute | solution.py:301
  37.5 20.2 %collective-permute-start.16 = (bf16[64,2176]{1,0:T(8,128)(2,1)S(1)}, bf16[64,2176]{1,0:T(8,128)(2,1)S(1)}, u32[]{:S(2)}, u32[]{:S(2)}) collective-permute-start(bf16[64,2176]{1,0:T(8,128)(2,1)S(1)} %collective-permute-done.3.refs_7_), channel_id=1, source_target_pairs={{0,2},{2,0},{4,6},{6,4},{8,10},{10,8},{12,14},{14,12},{16,18},{18,... | collective-permute-start | bytes 835592 | tf_op jit(solution)/shard_map/ppermute | solution.py:301
  53.1 14.5 %collective-permute-start.17 = (bf16[256,1024]{1,0:T(8,128)(2,1)}, bf16[256,1024]{1,0:T(8,128)(2,1)S(1)}, u32[]{:S(2)}, u32[]{:S(2)}) collective-permute-start(bf16[256,1024]{1,0:T(8,128)(2,1)} %param.26), channel_id=1, source_target_pairs={{0,1},{1,0},{2,3},{3,2},{4,5},{5,4},{6,7},{7,6},{8,9},{9,8},{10,11... | collective-permute-start | bytes 1572872 | tf_op jit(solution)/shard_map/ppermute | solution.py:368
  55.4 10.5 %collective-permute-start.7 = (bf16[64,2176]{1,0:T(8,128)(2,1)S(1)}, bf16[64,2176]{1,0:T(8,128)(2,1)S(1)}, u32[]{:S(2)}, u32[]{:S(2)}) collective-permute-start(bf16[64,2176]{1,0:T(8,128)(2,1)S(1)} %collective-permute-done.6.refs_3_), channel_id=1, source_target_pairs={{0,8},{2,10},{4,0},{6,2},{8,16},{10,18},{12,4},{14,6},{16,24},{18,... | collective-permute-start | bytes 835592 | tf_op jit(solution)/shard_map/ppermute | solution.py:301
  57.4 11.5 %collective-permute-start.15 = (bf16[64,2176]{1,0:T(8,128)(2,1)S(1)}, bf16[64,2176]{1,0:T(8,128)(2,1)S(1)}, u32[]{:S(2)}, u32[]{:S(2)}) collective-permute-start(bf16[64,2176]{1,0:T(8,128)(2,1)S(1)} %collective-permute-done.4.refs_6_), channel_id=1, source_target_pairs={{0,2},{2,0},{4,6},{6,4},{8,10},{10,8},{12,14},{14,12},{16,18},{18,... | collective-permute-start | bytes 835592 | tf_op jit(solution)/shard_map/ppermute | solution.py:301
  57.7 11.2 %collective-permute-start.11 = (bf16[64,2176]{1,0:T(8,128)(2,1)S(1)}, bf16[64,2176]{1,0:T(8,128)(2,1)S(1)}, u32[]{:S(2)}, u32[]{:S(2)}) collective-permute-start(bf16[64,2176]{1,0:T(8,128)(2,1)S(1)} %collective-permute-done.2.refs_2_), channel_id=1, source_target_pairs={{0,2},{2,0},{4,6},{6,4},{8,10},{10,8},{12,14},{14,12},{16,18},{18,... | collective-permute-start | bytes 835592 | tf_op jit(solution)/shard_map/ppermute | solution.py:301
  58.0 10.9 %collective-permute-start.14 = (bf16[64,2176]{1,0:T(8,128)(2,1)S(1)}, bf16[64,2176]{1,0:T(8,128)(2,1)S(1)}, u32[]{:S(2)}, u32[]{:S(2)}) collective-permute-start(bf16[64,2176]{1,0:T(8,128)(2,1)S(1)} %collective-permute-done.8.refs_5_), channel_id=1, source_target_pairs={{0,2},{2,0},{4,6},{6,4},{8,10},{10,8},{12,14},{14,12},{16,18},{18,... | collective-permute-start | bytes 835592 | tf_op jit(solution)/shard_map/ppermute | solution.py:301
  88.0 25.6 %collective-permute-start.18 = (bf16[512,1024]{1,0:T(8,128)(2,1)}, bf16[512,1024]{1,0:T(8,128)(2,1)}, u32[]{:S(2)}, u32[]{:S(2)}) collective-permute-start(bf16[512,1024]{1,0:T(8,128)(2,1)} %convolution_convert_fusion.2), channel_id=1, source_target_pairs={{0,1},{1,0},{2,3},{3,2},{4,5},{5,4},{6,7},{7,6},{8,9},{9,8},{10,11... | collective-permute-start | bytes 3145736 | tf_op jit(solution)/shard_map/ppermute | solution.py:368
  146.8 24.8 %collective-permute-start.19 = (bf16[512,1024]{1,0:T(8,128)(2,1)}, bf16[512,1024]{1,0:T(8,128)(2,1)}, u32[]{:S(2)}, u32[]{:S(2)}) collective-permute-start(bf16[512,1024]{1,0:T(8,128)(2,1)} %get-tuple-element.137), channel_id=1, source_target_pairs={{0,1},{1,0},{2,3},{3,2},{4,5},{5,4},{6,7},{7,6},{8,9},{9,8},{10,11... | collective-permute-start | bytes 3145736 | tf_op jit(solution)/shard_map/ppermute | solution.py:368
  217.2 9.9 %collective-permute-start.24 = (bf16[64,2176]{1,0:T(8,128)(2,1)}, bf16[64,2176]{1,0:T(8,128)(2,1)}, u32[]{:S(2)}, u32[]{:S(2)}) collective-permute-start(bf16[64,2176]{1,0:T(8,128)(2,1)} %get-tuple-element.109), channel_id=1, source_target_pairs={{0,8},{2,10},{4,0},{6,2},{8,16},{10,18},{12,4},{14,6},{16,24},{18,... | collective-permute-start | bytes 835592 | tf_op jit(solution)/shard_map/ppermute | solution.py:301
  217.2 11.1 %collective-permute-start.23 = (bf16[64,2176]{1,0:T(8,128)(2,1)}, bf16[64,2176]{1,0:T(8,128)(2,1)}, u32[]{:S(2)}, u32[]{:S(2)}) collective-permute-start(bf16[64,2176]{1,0:T(8,128)(2,1)} %get-tuple-element.110), channel_id=1, source_target_pairs={{0,4},{2,6},{4,12},{6,14},{8,0},{10,2},{12,20},{14,22},{16,8},{18,... | collective-permute-start | bytes 835592 | tf_op jit(solution)/shard_map/ppermute | solution.py:301
  221.1 15.1 %collective-permute-start.20 = (bf16[256,1024]{1,0:T(8,128)(2,1)}, bf16[256,1024]{1,0:T(8,128)(2,1)}, u32[]{:S(2)}, u32[]{:S(2)}) collective-permute-start(bf16[256,1024]{1,0:T(8,128)(2,1)} %constant_dynamic-slice_fusion.2), channel_id=1, source_target_pairs={{0,1},{1,0},{2,3},{3,2},{4,5},{5,4},{6,7},{7,6},{8,9},{9,8},{10,11... | collective-permute-start | bytes 1572872 | tf_op jit(solution)/shard_map/ppermute | solution.py:368
  229.0 25.4 %collective-permute-start.25 = (bf16[256,1024]{1,0:T(8,128)(2,1)}, bf16[256,1024]{1,0:T(8,128)(2,1)}, u32[]{:S(2)}, u32[]{:S(2)}) collective-permute-start(bf16[256,1024]{1,0:T(8,128)(2,1)} %constant_dynamic-slice_fusion.1), channel_id=1, source_target_pairs={{0,1},{1,0},{2,3},{3,2},{4,5},{5,4},{6,7},{7,6},{8,9},{9,8},{10,11... | collective-permute-start | bytes 1572872 | tf_op jit(solution)/shard_map/ppermute | solution.py:368
  232.1 16.9 %collective-permute-start.26 = (bf16[64,2176]{1,0:T(8,128)(2,1)}, bf16[64,2176]{1,0:T(8,128)(2,1)S(1)}, u32[]{:S(2)}, u32[]{:S(2)}) collective-permute-start(bf16[64,2176]{1,0:T(8,128)(2,1)} %get-tuple-element.46), channel_id=1, source_target_pairs={{0,4},{2,6},{4,12},{6,14},{8,0},{10,2},{12,20},{14,22},{16,8},{18,... | collective-permute-start | bytes 835592 | tf_op jit(solution)/shard_map/ppermute | solution.py:301
  234.5 14.4 %collective-permute-start.27 = (bf16[64,2176]{1,0:T(8,128)(2,1)}, bf16[64,2176]{1,0:T(8,128)(2,1)S(1)}, u32[]{:S(2)}, u32[]{:S(2)}) collective-permute-start(bf16[64,2176]{1,0:T(8,128)(2,1)} %get-tuple-element.47), channel_id=1, source_target_pairs={{0,8},{2,10},{4,0},{6,2},{8,16},{10,18},{12,4},{14,6},{16,24},{18,... | collective-permute-start | bytes 835592 | tf_op jit(solution)/shard_map/ppermute | solution.py:301
  252.4 8.3 %collective-permute-start.28 = (bf16[64,2176]{1,0:T(8,128)(2,1)}, bf16[64,2176]{1,0:T(8,128)(2,1)}, u32[]{:S(2)}, u32[]{:S(2)}) collective-permute-start(bf16[64,2176]{1,0:T(8,128)(2,1)} %get-tuple-element.48), channel_id=1, source_target_pairs={{0,4},{2,6},{4,12},{6,14},{8,0},{10,2},{12,20},{14,22},{16,8},{18,... | collective-permute-start | bytes 835592 | tf_op jit(solution)/shard_map/ppermute | solution.py:301
  253.7 12.5 %collective-permute-start.30 = (bf16[64,2176]{1,0:T(8,128)(2,1)}, bf16[64,2176]{1,0:T(8,128)(2,1)}, u32[]{:S(2)}, u32[]{:S(2)}) collective-permute-start(bf16[64,2176]{1,0:T(8,128)(2,1)} %get-tuple-element.49), channel_id=1, source_target_pairs={{0,8},{2,10},{4,0},{6,2},{8,16},{10,18},{12,4},{14,6},{16,24},{18,... | collective-permute-start | bytes 835592 | tf_op jit(solution)/shard_map/ppermute | solution.py:301
  (48 other events, 321.0 us)
Sparse Core Ops, SparseCore 0:
  25.9 78.4 all-gather.1
  140.1 109.8 reduce-scatter.1
where the time goes:
time: 286 us; the launch traced here: 285 us
  waiting for transfers between devices  106 us (37%)
  matrix products  45.9 us (16%)
  Pallas kernels  38.8 us (14%)
  other arithmetic  27.7 us (10%)
  starting transfers between devices  27.2 us (10%)
  local copies, waits for them, and re-layouts  24.4 us (9%)
  between operations  14.8 us (5%)
    ppermute x23, waiting for transfers between devices, hop(): return lax.ppermute(value, 'fsdp', pairs)  63.1 us
    dot_general x13, matrix products, dot(): lax.dot_general(left, right, (dims, ((), ())), preferred_element_type=F32)  45.9 us
    ppermute x8, waiting for transfers between devices, swap(): return lax.ppermute(value, 'tensor', [(0, 1), (1, 0)])  43.2 us
    ppermute x23, starting transfers between devices, hop(): return lax.ppermute(value, 'fsdp', pairs)  15.3 us
    unnamed x86, local copies, waits for them, and re-layouts  12.3 us
    ppermute x8, starting transfers between devices, swap(): return lax.ppermute(value, 'tensor', [(0, 1), (1, 0)])  11.9 us
    pallas_call x1, Pallas kernels, paired_products(): pl.pallas_call(multiply, grid=(2 * half,), in_specs=[whole, whole, pl.Blo...  10.1 us
    pallas_call x1, Pallas kernels, attend_back(): pl.pallas_call(backward, grid=(seq_count, width // step), in_specs=[pl.Bl...  9.65 us
  transfers between devices with their start and end apart: 33, of which 17 were waited for; matrix products, arithmetic and copies ran while one was open for 26% of the time, Pallas kernels for 10%

commit v1 on v0

--- a/solution.py
+++ b/solution.py
@@ -50,19 +50,24 @@
     return lax.optimization_barrier(values)
 
 
-def assemble(table, pieces):
-    m, n = pieces[0].shape
+def assemble(table, pieces, m):
+    n = pieces[0].shape[1]
     count = len(pieces)
+    total = sum(piece.shape[0] for piece in pieces)
 
     def copy(places, *refs):
+        j = 0
         for i in range(count):
-            refs[count][pl.ds(pl.multiple_of(places[i] * m, m), m), :] = refs[i][...]
+            for own in range(pieces[i].shape[0] // m):
+                rows = pl.ds(pl.multiple_of(places[j] * m, m), m)
+                refs[count][rows, :] = refs[i][own * m : (own + 1) * m, :]
+                j += 1
 
     return pl.pallas_call(
         copy,
         in_specs=[pl.BlockSpec(memory_space=pltpu.SMEM)]
         + [pl.BlockSpec(memory_space=pltpu.VMEM)] * count,
-        out_shape=jax.ShapeDtypeStruct((count * m, n), pieces[0].dtype),
+        out_shape=jax.ShapeDtypeStruct((total, n), pieces[0].dtype),
         compiler_params=pltpu.CompilerParams(vmem_limit_bytes=VMEM_LIMIT),
         name="assemble",
     )(table, *pieces)
@@ -95,68 +100,47 @@
     )(table, *arrays)
 
 
-def ring_add(own, numbers, arrived):
-    lanes = len(numbers)
-    shape = arrived[0].shape
-
-    def add(*refs):
-        for j in range(lanes):
-            total = refs[j][...].astype(F32) + refs[lanes + j][...].astype(F32)
-            refs[2 * lanes + j][...] = total.astype(BF16)
-
-    blocks = [pl.BlockSpec(shape, lambda i, k=k: (k, 0)) for k in numbers]
-    whole = pl.BlockSpec(shape, lambda i: (0, 0))
-    return pl.pallas_call(
-        add,
-        grid=(1,),
-        in_specs=blocks + [whole] * lanes,
-        out_specs=[whole] * lanes,
-        out_shape=[jax.ShapeDtypeStruct(shape, BF16)] * lanes,
-        name="ring_add",
-    )(*[own] * lanes, *arrived)
-
-
-def paired_products(lefts, rights):
+def paired_products(table, lefts, rights, m):
     depth, rows = lefts[0].shape
     width = rights[0].shape[1]
     tile = min(width, 512)
     half = width // tile
 
-    def multiply(left_a, left_b, right_a, right_b, target, turned):
+    def multiply(places, left_a, left_b, right_a, right_b, own, away, raw, turned):
         j = pl.program_id(0)
 
-        @pl.when(j == 0)
-        def _():
-            turned[...] = left_a[...].T
-
-        @pl.when(j == half)
-        def _():
-            turned[...] = left_b[...].T
-
-        @pl.when(j < half)
-        def _():
-            target[...] = dot(turned[...], right_a[...], ((1,), (0,))).astype(BF16)
-
-        @pl.when(j >= half)
-        def _():
-            target[...] = dot(turned[...], right_b[...], ((1,), (0,))).astype(BF16)
+        def turn(left):
+            raw[...] = left[...].T
+            for i in range(rows // m):
+                block = pl.ds(pl.multiple_of(places[i] * m, m), m)
+                turned[i * m : (i + 1) * m, :] = raw[block, :]
+
+        def product(right):
+            own[...] = dot(turned[: rows // 2], right[...], ((1,), (0,))).astype(BF16)
+            away[...] = dot(turned[rows // 2 :], right[...], ((1,), (0,))).astype(BF16)
+
+        pl.when(j == 0)(lambda: turn(left_a))
+        pl.when(j == half)(lambda: turn(left_b))
+        pl.when(j < half)(lambda: product(right_a))
+        pl.when(j >= half)(lambda: product(right_b))
 
     whole = pl.BlockSpec((depth, rows), lambda j: (0, 0))
     return pl.pallas_call(
         multiply,
         grid=(2 * half,),
         in_specs=[
+            pl.BlockSpec(memory_space=pltpu.SMEM),
             whole,
             whole,
             pl.BlockSpec((depth, tile), lambda j: (0, jnp.minimum(j, half - 1))),
             pl.BlockSpec((depth, tile), lambda j: (0, jnp.maximum(j - half, 0))),
         ],
-        out_specs=pl.BlockSpec((rows, tile), lambda j: (0, j)),
-        out_shape=jax.ShapeDtypeStruct((rows, 2 * width), BF16),
-        scratch_shapes=[pltpu.VMEM((rows, depth), BF16)],
+        out_specs=[pl.BlockSpec((rows // 2, tile), lambda j: (0, j))] * 2,
+        out_shape=[jax.ShapeDtypeStruct((rows // 2, 2 * width), BF16)] * 2,
+        scratch_shapes=[pltpu.VMEM((rows, depth), BF16)] * 2,
         compiler_params=pltpu.CompilerParams(vmem_limit_bytes=VMEM_LIMIT),
         name="paired_products",
-    )(*lefts, *rights)
+    )(table, *lefts, *rights)
 
 
 def allowed_pairs(column, row):
@@ -289,9 +273,23 @@
             back = [self.cycle[(self.place[chip] - k) % self.chips] for k in range(self.chips)]
             rows.append([2 * c + core for c in back] + [2 * c + 1 - core for c in back])
         self.tables = np.asarray(rows, np.int32)
+        along = [[2 * chip + core for chip in self.cycle] for core in range(2)]
+        self.groups = along
+        self.places = np.asarray([along[0] + along[1], along[1] + along[0]], np.int32)
 
     def table(self):
         return jnp.asarray(self.tables)[lax.axis_index("fsdp")]
+
+    def along(self):
+        return jnp.asarray(self.places)[lax.axis_index("fsdp") % 2]
+
+    def gather(self, block):
+        return lax.all_gather(block, "fsdp", axis=0, tiled=True, axis_index_groups=self.groups)
+
+    def scatter(self, own):
+        return lax.psum_scatter(
+            own, "fsdp", scatter_dimension=0, tiled=True, axis_index_groups=self.groups
+        )
 
     def hop(self, value, core=0, along=0):
         pairs = []
@@ -320,44 +318,8 @@
         while len(self.up) <= self.ring.chips // 2:
             self.step()
         own = self.up + self.down[:0:-1]
-        return assemble(table, own + [self.ring.hop(piece, core=1) for piece in own])
-
-
-class Scatter:
-    def __init__(self, ring, table, sums):
-        self.ring = ring
-        self.chips = ring.chips
-        self.widths = [own.shape[1] for own in sums]
-        self.m = sums[0].shape[0] // ring.size
-        away = row_blocks(table, sums, range(self.chips, 2 * self.chips), self.m)
-        arrived = ring.hop(away, core=1)
-        self.own = row_blocks(table, sums, range(self.chips), self.m, arrived)
-        self.up = self.down = None
-        self.done = 0
-
-    def step(self):
-        numbers = [self.chips // 2 - self.done]
-        if self.chips // 2 + 1 + self.done < self.chips:
-            numbers.append(self.chips // 2 + 1 + self.done)
-        if self.done:
-            moved = ring_add(self.own, numbers, [self.up, self.down][: len(numbers)])
-        else:
-            moved = [self.own[k * self.m : (k + 1) * self.m] for k in numbers]
-        self.up = self.ring.hop(moved[0], along=-1)
-        if len(numbers) > 1:
-            self.down = self.ring.hop(moved[1], along=1)
-        self.done += 1
-
-    def before(self, *values):
-        values = tie(*values, self.up, self.down)[: len(values)]
-        return values if len(values) > 1 else values[0]
-
-    def totals(self):
-        while self.done < self.chips // 2:
-            self.step()
-        total = self.own[: self.m].astype(F32) + self.up.astype(F32) + self.down.astype(F32)
-        ends = np.cumsum(self.widths)
-        return [total[:, end - n : end] for n, end in zip(self.widths, ends)]
+        m = own[0].shape[0]
+        return assemble(table, own + [self.ring.hop(piece, core=1) for piece in own], m)
 
 
 class Pair:
@@ -382,7 +344,7 @@
             return lax.psum(rounded.astype(F32), "tensor")
         return rounded.astype(F32) + self.swap(rounded).astype(F32)
 
-    def collect(self, partial_rows):
+    def collect(self, partial_rows, after=None):
         rounded = partial_rows.astype(BF16)
         if self.size != 2:
             return lax.psum_scatter(rounded, "tensor", scatter_dimension=0, tiled=True).astype(F32)
@@ -390,7 +352,10 @@
         index = lax.axis_index("tensor")
         away = lax.dynamic_slice_in_dim(rounded, (1 - index) * rows, rows, 0)
         stay = lax.dynamic_slice_in_dim(rounded, index * rows, rows, 0)
-        return stay.astype(F32) + self.swap(away).astype(F32)
+        other = self.swap(away)
+        if after is not None:
+            other, _ = tie(other, after)
+        return stay.astype(F32) + other.astype(F32)
 
     def sum(self, terms):
         if self.size != 2:
@@ -429,6 +394,7 @@
         q_len, h_len = query_bias.size, hidden_bias.size
 
         table = ring.table()
+        along = ring.along()
         six = pair.spread(jnp.concatenate([norm_gains, row_biases], axis=0).T)
         head_flat = jnp.concatenate(
             [query_bias.reshape(q_len), value_bias.reshape(q_len), hidden_bias.reshape(h_len)]
@@ -448,10 +414,8 @@
         )
         one.step()
         hidden_block = jnp.concatenate([hidden_in, hidden_out.T], axis=1)
-        hidden_block = one.before(hidden_block)
-        hidden_full = lax.all_gather(hidden_block, "fsdp", axis=0, tiled=True)
-        up_full, down_t = hidden_full[:, :hidden_width], hidden_full[:, hidden_width:]
         one.step()
+        hidden_half = ring.gather(one.before(hidden_block))
         tok_rows = pair.spread(one.before(tokens)).astype(F32)
         one.step()
         grad_all = pair.spread(one.before(output_grad))
@@ -488,7 +452,11 @@
         value_rows = (projected[:, 2 * local_width :] + value_add).astype(BF16)
         query_rows, grad_all = tie(query_rows, grad_all)
         mixed_rows = attend(query_rows, key_rows, value_rows, segments, score_scale)
-        attn_rows = pair.total(dot(mixed_rows, out_t, ((1,), (1,))))
+        attn_part = dot(mixed_rows, out_t, ((1,), (1,))).astype(BF16)
+        hidden_half, _ = tie(hidden_half, attn_part)
+        attn_rows = pair.total(attn_part)
+        hidden_full = assemble(along, [hidden_half, ring.hop(hidden_half, core=1)], m)
+        up_full, down_t = hidden_full[:, :hidden_width], hidden_full[:, hidden_width:]
         resid_rows = tok_rows + attn_rows + biases_all[1]
         normed_two, inverse_two = normalize(resid_rows)
         in_two = (normed_two * gains_all[1] + biases_all[2]).astype(BF16)
@@ -499,26 +467,31 @@
         g_pre = dot(grad_all, down_t, ((1,), (0,))) * slope
         g_hidden_add = jnp.sum(g_pre, axis=0)
         g_pre_b = g_pre.astype(BF16)
-        g_hidden = paired_products([grad_all, in_two], [act_rows, g_pre_b])
-        g_pre_b, act_rows, g_hidden = tie(g_pre_b, act_rows, g_hidden)
+        hidden_own, hidden_away = paired_products(
+            along, [grad_all, in_two], [act_rows, g_pre_b], m
+        )
+        g_pre_b, act_rows, hidden_away = tie(g_pre_b, act_rows, hidden_away)
         g_two_part = dot(g_pre_b, up_full, ((1,), (1,)))
         g_norm_two = pair.total(g_two_part)
-        g_hidden_own = lax.psum_scatter(g_hidden, "fsdp", scatter_dimension=0, tiled=True)
-        g_down_t, g_up = g_hidden_own[:, :hidden_width], g_hidden_own[:, hidden_width:]
+        hidden_own = hidden_own.astype(F32) + ring.hop(hidden_away, core=1).astype(F32)
+        hidden_own = hidden_own.astype(BF16)
+        g_hidden_own = ring.scatter(hidden_own)
         mlp_part = dot(act_rows, down_t, ((1,), (1,)))
-        g_norm_two, mlp_part = tie(g_norm_two, mlp_part.astype(BF16))
-        mlp_rows = pair.collect(mlp_part)
-        result = (pair.own(resid_rows) + mlp_rows + biases_all[3]).astype(BF16)
+        mlp_part = mlp_part.astype(BF16)
+        g_norm_two, _, _ = tie(g_norm_two, mlp_part, hidden_own)
 
         grad_rows = grad_all.astype(F32)
         g_resid = grad_rows + normalize_back(g_norm_two, normed_two, inverse_two, gains_all[1])
         g_resid_b = g_resid.astype(BF16)
         g_mixed = dot(g_resid_b, out_t, ((1,), (0,))).astype(BF16)
+        mlp_rows = pair.collect(mlp_part, g_mixed)
+        result = (pair.own(resid_rows) + mlp_rows + biases_all[3]).astype(BF16)
         g_query, g_keys, g_values, g_query_add, g_value_add = attend_back(
             query_rows, key_rows, value_rows, g_mixed, segments, score_scale
         )
         g_query_add = jnp.sum(g_query_add, axis=0)
         g_value_add = jnp.sum(g_value_add, axis=0)
+        g_query, result = tie(g_query, result)
         g_proj = jnp.concatenate([g_query, g_keys, g_values], axis=1)
         g_one_part = dot(g_proj, in_full, ((1,), (1,)))
 
@@ -556,25 +529,27 @@
         spots = jnp.asarray(np.arange(6 + head_count)[:, None] == lanes, BF16)
         small = dot(small, spots, ((0,), (0,))).astype(BF16)
 
-        outer = Scatter(
-            ring,
-            table,
-            [
-                dot(in_one, g_proj, ((0,), (0,))).astype(BF16),
-                dot(g_resid_b, mixed_rows, ((0,), (0,))).astype(BF16),
-                small,
-            ],
-        )
-        outer.step()
-        g_one_part = outer.before(g_one_part.astype(BF16))
+        sums = [
+            dot(in_one, g_proj, ((0,), (0,))).astype(BF16),
+            dot(g_resid_b, mixed_rows, ((0,), (0,))).astype(BF16),
+            small,
+        ]
+        away = row_blocks(along, sums, range(ring.chips, 2 * ring.chips), m)
+        arrived = ring.hop(away, core=1)
+        outer_own = row_blocks(along, sums, range(ring.chips), m, arrived)
+        g_one_part, _ = tie(g_one_part.astype(BF16), outer_own)
+        outer_own, g_hidden_own = tie(outer_own, g_hidden_own)
+        outer_own = ring.scatter(outer_own)
         g_norm_one = pair.collect(g_one_part)
-        outer.step()
         tokens_grad = (
             pair.own(g_resid)
             + normalize_back(g_norm_one, pair.own(normed_one), pair.own(inverse_one), gains_all[0])
         ).astype(BF16)
-        g_in, g_out_t, small = outer.totals()
-        small = small.T
+        g_down_t, g_up = g_hidden_own[:, :hidden_width], g_hidden_own[:, hidden_width:]
+        outer_own = outer_own.astype(F32)
+        g_in = outer_own[:, : 3 * local_width]
+        g_out_t = outer_own[:, 3 * local_width : 4 * local_width]
+        small = outer_own[:, 4 * local_width :].T
         six_sum = lax.dynamic_slice_in_dim(
             small[:6], lax.axis_index("tensor") * (m // n_tensor), m // n_tensor, 1
         )

time: 286 us -> 285 us (level)
  waiting for transfers between devices: 106 us -> 114 us
  starting transfers between devices: 27.2 us -> 19.6 us
    ppermute x23 -> x18, waiting for transfers between devices: 63.1 us -> 41.1 us  [hop(): return lax.ppermute(value, 'fsdp', pairs)]
    ppermute x8, waiting for transfers between devices: 43.2 us -> 55.7 us  [swap(): return lax.ppermute(value, 'tensor', [(0, 1), (1, 0)])]
    reduce_scatter x1 -> x2, waiting for transfers between devices: 0.01 us -> 11.9 us  [scatter(): lax.psum_scatter(own, 'fsdp', scatter_dimension=0, tiled=True, axis_index...]
    ppermute x23 -> x18, starting transfers between devices: 15.3 us -> 8.16 us  [hop(): return lax.ppermute(value, 'fsdp', pairs)]
    convert_element_type x0 -> x2, other arithmetic: none -> 6.39 us  [the longest x1 5.4 us: shards(): hidden_own = hidden_own.astype(BF16)]
    pallas_call x1 -> x2, Pallas kernels: 2.91 us -> 8.99 us  [assemble(): pl.pallas_call(copy, in_specs=[pl.BlockSpec(memory_space=pltpu.SMEM)] + [...]
    pallas_call x4 -> x1, Pallas kernels: 16 us -> 10.1 us  [paired_products(): pl.pallas_call(multiply, grid=(2 * half,), in_specs=[pl.BlockSpec(memory_...]
    all_gather x1, waiting for transfers between devices: 0.01 us -> 5.66 us  [gather(): lax.all_gather(block, 'fsdp', axis=0, tiled=True, axis_index_groups=self....]
  transfers between devices with their start and end apart: 33 -> 29, of which waited for: 17 -> 14; matrix products, arithmetic and copies ran while one was open for 26% -> 22% of each run, Pallas kernels for 10% -> 9%
where the time goes in v1:
time: 285 us; the launch traced here: 284 us
  waiting for transfers between devices  114 us (40%)
  matrix products  44.4 us (16%)
  Pallas kernels  40.6 us (14%)
  other arithmetic  29 us (10%)
  local copies, waits for them, and re-layouts  21.7 us (8%)
  starting transfers between devices  19.6 us (7%)
  between operations  14.6 us (5%)
    ppermute x8, waiting for transfers between devices, swap(): return lax.ppermute(value, 'tensor', [(0, 1), (1, 0)])  55.7 us
    dot_general x13, matrix products, dot(): lax.dot_general(left, right, (dims, ((), ())), preferred_element_type=F32)  44.4 us
    ppermute x18, waiting for transfers between devices, hop(): return lax.ppermute(value, 'fsdp', pairs)  41.1 us
    reduce_scatter x2, waiting for transfers between devices, scatter(): lax.psum_scatter(own, 'fsdp', scatter_dimension=0, tiled=True, axis_index...  11.9 us
    ppermute x8, starting transfers between devices, swap(): return lax.ppermute(value, 'tensor', [(0, 1), (1, 0)])  11.1 us
    unnamed x84, local copies, waits for them, and re-layouts  11 us
    pallas_call x1, Pallas kernels, paired_products(): pl.pallas_call(multiply, grid=(2 * half,), in_specs=[pl.BlockSpec(memory_...  10.1 us
    pallas_call x1, Pallas kernels, attend_back(): pl.pallas_call(backward, grid=(seq_count, width // step), in_specs=[pl.Bl...  9.68 us
  transfers between devices with their start and end apart: 29, of which 14 were waited for; matrix products, arithmetic and copies ran while one was open for 22% of the time, Pallas kernels for 9%

profile of v1, /device:TPU:0, one launch (start us, length us, event | category | flops | bytes accessed | tf_op | source)
XLA Modules:
  0.0 284.1 jit_solution(17620014382139301724)
XLA Ops:
  18.4 6.1 %collective-permute-done.3.refs_7_ = bf16[64,2176]{1,0:T(8,128)(2,1)S(1)} collective-permute-done((bf16[64,2176]{1,0:T(8,128)(2,1)S(1)}, bf16[64,2176]{1,0:T(8,128)(2,1)S(1)}, u32[]{:S(2)}, u32[]{:S(2)}) %collective-permute-start.3) | collective-permute-done | bytes 278560 | tf_op jit(solution)/shard_map/ppermute | solution.py:299
  28.4 3.3 %collective-permute-done.4.refs_6_ = bf16[64,2176]{1,0:T(8,128)(2,1)S(1)} collective-permute-done((bf16[64,2176]{1,0:T(8,128)(2,1)S(1)}, bf16[64,2176]{1,0:T(8,128)(2,1)S(1)}, u32[]{:S(2)}, u32[]{:S(2)}) %collective-permute-start.4) | collective-permute-done | bytes 278560 | tf_op jit(solution)/shard_map/ppermute | solution.py:299
  37.0 4.0 %collective-permute-done.8.refs_5_ = bf16[64,2176]{1,0:T(8,128)(2,1)S(1)} collective-permute-done((bf16[64,2176]{1,0:T(8,128)(2,1)S(1)}, bf16[64,2176]{1,0:T(8,128)(2,1)S(1)}, u32[]{:S(2)}, u32[]{:S(2)}) %collective-permute-start.8) | collective-permute-done | bytes 278560 | tf_op jit(solution)/shard_map/ppermute | solution.py:299
  49.5 11.4 %collective-permute-done.7.refs_4_ = bf16[64,2176]{1,0:T(8,128)(2,1)S(1)} collective-permute-done((bf16[64,2176]{1,0:T(8,128)(2,1)S(1)}, bf16[64,2176]{1,0:T(8,128)(2,1)S(1)}, u32[]{:S(2)}, u32[]{:S(2)}) %collective-permute-start.7) | collective-permute-done | bytes 278560 | tf_op jit(solution)/shard_map/ppermute | solution.py:299
  68.5 4.2 %fusion.10 = f32[512,1536]{1,0:T(8,128)S(1)} fusion(bf16[1024,2176]{1,0:T(8,128)(2,1)} %assemble.2, f32[1024]{0:T(1024)S(1)} %bitcast.107, f32[1024]{0:T(1024)S(1)} %bitcast.92, f32[512]{0:T(512)S(1)} %add_rsqrt_fusion.1, f32[512]{0:T(512)S(1)} %broadcast_multiply_fusion.3, bf16[256,1024]{1,0:T(8,128)(2,1)} %copy-done.16, bf16[256,1024]{1,0:T(8,128)(2,1)} %copy-done.14), kind=kOutput, calls=%fused_computation.19 | convolution fusion | flops 1615331328 | bytes 7352320 | tf_op jit(solution)/shard_map/dot_general | solution.py:246
  73.0 5.9 %attend.1 = bf16[512,512]{1,0:T(8,128)(2,1)S(1)} custom-call(s32[512,1]{1,0:T(8,128)S(1)} %copy.100.column, s32[1,1,512]{2,1,0:T(1,128)S(1)} %bitcast.71, bf16[512,512]{1,0:T(8,128)(2,1)S(1)} %get-tuple-element.36.query, bf16[512,512]{1,0:T(8,128)(2,1)S(1)} %slice.199.key, bf16[512,512]{1,0:T(8,128)(2,1)S(1)} %get-tuple-element.113.value), custom_call_target="tpu_custom_call" | custom-call | tf_op jit(solution)/shard_map/attend/pallas_call | solution.py:171
  82.0 5.7 %all-gather.2.cloned.1.call-done.refs_0_ = bf16[512,4096]{1,0:T(8,128)(2,1)} async-done(((bf16[64,4096]{1,0:T(8,128)(2,1)}), bf16[512,4096]{1,0:T(8,128)(2,1)}) %all-gather.2.cloned.1.call-update) | async-done | bytes 4194320 | tf_op jit(solution)/shard_map/all_gather | solution.py:287
  89.5 24.0 %collective-permute-done.18 = bf16[512,1024]{1,0:T(8,128)(2,1)} collective-permute-done((bf16[512,1024]{1,0:T(8,128)(2,1)}, bf16[512,1024]{1,0:T(8,128)(2,1)}, u32[]{:S(2)}, u32[]{:S(2)}) %collective-permute-start.18) | collective-permute-done | bytes 1048608 | tf_op jit(solution)/shard_map/ppermute | solution.py:330
  118.9 6.0 %assemble.3 = bf16[1024,4096]{1,0:T(8,128)(2,1)} custom-call(s32[16]{0:T(128)S(1)} %fusion.36.places, bf16[512,4096]{1,0:T(8,128)(2,1)S(1)} %copy-done, bf16[512,4096]{1,0:T(8,128)(2,1)} %collective-permute-done.19.refs_1_), custom_call_target="tpu_custom_call" | custom-call | tf_op jit(solution)/shard_map/assemble/pallas_call | solution.py:66
  124.9 5.3 %multiply_convert_fusion = (bf16[512,2048]{1,0:T(8,128)(2,1)S(1)}, f32[512,2048]{1,0:T(8,128)S(1)}) fusion(f32[2048]{0:T(1024)S(1)} %add.188, bf16[512,1024]{1,0:T(8,128)(2,1)S(1)} %add_convert_fusion.1.left_b, bf16[1024,4096]{1,0:T(8,128)(2,1)} %assemble.3), kind=kOutput, calls=%fused_computation.1 | convolution fusion | flops 2157969408 | bytes 11542528 | tf_op jit(solution)/shard_map/dot_general | solution.py:246
  130.2 5.6 %fusion.42 = (bf16[2048]{0:T(1024)(128)(2,1)S(1)}, bf16[512,2048]{1,0:T(8,128)(2,1)}) fusion(f32[512,2048]{1,0:T(8,128)S(1)} %get-tuple-element.140, f32[2048]{0:T(1024)S(1)} %add.188, bf16[512,1024]{1,0:T(8,128)(2,1)S(1)} %pad_maximum_fusion.1.left_a, bf16[1024,4096]{1,0:T(8,128)(2,1)S(1)} %copy-done.13), kind=kOutput, calls=%fused_computation.112 | convolution fusion | flops 2168453120 | bytes 11546624 | tf_op jit(solution)/shard_map/dot_general | solution.py:246
  135.8 10.1 %paired_products.1 = (bf16[512,4096]{1,0:T(8,128)(2,1)}, bf16[512,4096]{1,0:T(8,128)(2,1)}) custom-call(s32[16]{0:T(128)S(1)} %fusion.36.places, bf16[512,1024]{1,0:T(8,128)(2,1)S(1)} %pad_maximum_fusion.1.left_a, bf16[512,1024]{1,0:T(8,128)(2,1)S(1)} %add_convert_fusion.1.left_b, bf16[512,2048]{1,0:T(8,128)(2,1)S(1)} %get-tuple-element.42.right_a, ...), custom_call_target="tpu_custom_call" | custom-call | tf_op jit(solution)/shard_map/paired_products/pallas_call | solution.py:128
  146.0 7.4 %collective-permute-done.21 = bf16[512,4096]{1,0:T(8,128)(2,1)S(1)} collective-permute-done((bf16[512,4096]{1,0:T(8,128)(2,1)}, bf16[512,4096]{1,0:T(8,128)(2,1)S(1)}, u32[]{:S(2)}, u32[]{:S(2)}) %collective-permute-start.21) | collective-permute-done | bytes 4194336 | tf_op jit(solution)/shard_map/ppermute | solution.py:299
  153.3 5.4 %add_convert_fusion = bf16[512,4096]{1,0:T(8,128)(2,1)} fusion(bf16[512,4096]{1,0:T(8,128)(2,1)S(1)} %collective-permute-done.21, bf16[512,4096]{1,0:T(8,128)(2,1)} %get-tuple-element.43), kind=kLoop, calls=%fused_computation | loop fusion | flops 8388608 | bytes 12582912 | tf_op jit(solution)/shard_map/convert_element_type | solution.py:477
  159.0 6.8 %fusion.46 = (bf16[512,1024]{1,0:T(8,128)(2,1)}, f32[512,1024]{1,0:T(8,128)}) fusion(bf16[512,2048]{1,0:T(8,128)(2,1)} %get-tuple-element.41.right_b, bf16[1024,4096]{1,0:T(8,128)(2,1)} %assemble.3), kind=kOutput, calls=%fused_computation.116 | convolution fusion | flops 2148007936 | bytes 9437184 | tf_op jit(solution)/shard_map/dot_general | solution.py:246
  167.9 5.2 %fusion.18 = bf16[512,1024]{1,0:T(8,128)(2,1)S(1)} fusion(bf16[512,2048]{1,0:T(8,128)(2,1)} %copy-done.1, bf16[1024,4096]{1,0:T(8,128)(2,1)} %assemble.3), kind=kOutput, calls=%fused_computation.37 | convolution fusion | flops 2148007936 | bytes 7340032 | tf_op jit(solution)/shard_map/dot_general | solution.py:246
  173.8 18.4 %collective-permute-done.20 = bf16[512,1024]{1,0:T(8,128)(2,1)} collective-permute-done((bf16[512,1024]{1,0:T(8,128)(2,1)}, bf16[512,1024]{1,0:T(8,128)(2,1)}, u32[]{:S(2)}, u32[]{:S(2)}) %collective-permute-start.20) | collective-permute-done | bytes 1048608 | tf_op jit(solution)/shard_map/ppermute | solution.py:330
  199.2 9.7 %attend_back.1 = (bf16[512,512]{1,0:T(8,128)(2,1)S(1)}, bf16[512,512]{1,0:T(8,128)(2,1)S(1)}, bf16[512,512]{1,0:T(8,128)(2,1)S(1)}, f32[1,1,512]{2,1,0:T(1,128)S(1)}, f32[1,1,512]{2,1,0:T(1,128)S(1)}) custom-call(s32[512,1]{1,0:T(8,128)S(1)} %copy.100.column, s32[1,1,512]{2,1,0:T(1,128)S(1)} %bitcast.72, bf16[512,512]{1,0:T(8,128)(2,1)S(1)} %get-tuple-element.36.query, ...), custom_call_target="tpu_custom_call" | custom-call | tf_op jit(solution)/shard_map/attend_back/pallas_call | solution.py:220
  215.0 6.1 %fusion.39 = (f32[1024]{0:T(1024)S(1)}, f32[1024]{0:T(1024)S(1)}, bf16[512,1024]{1,0:T(8,128)(2,1)}, f32[512,1024]{1,0:T(8,128)}) fusion(f32[512]{0:T(512)S(1)} %copy-done.31, f32[512]{0:T(512)S(1)} %copy-done.29, bf16[256,1024]{1,0:T(8,128)(2,1)S(1)} %copy-done.17, bf16[256,1024]{1,0:T(8,128)(2,1)S(1)} %copy-done.15, ...), kind=kOutput, calls=%fused_computation.110 | convolution fusion | flops 1615853568 | bytes 8925184 | tf_op jit(solution)/shard_map/dot_general | solution.py:246
  223.6 3.7 %convolution_convert_fusion.refs_0_ = bf16[1024,1536]{1,0:T(8,128)(2,1)} fusion(bf16[512,1536]{1,0:T(8,128)(2,1)S(1)} %copy-done.25, f32[1024]{0:T(1024)S(1)} %bitcast.108, f32[1024]{0:T(1024)S(1)} %bitcast.93, f32[512]{0:T(512)S(1)} %copy-done.31, f32[512]{0:T(512)S(1)} %copy-done.29, bf16[256,1024]{1,0:T(8,128)(2,1)S(1)} %copy-done.18, ...), kind=kOutput, calls=%fused_computation.5 | convolution fusion | flops 1616904192 | bytes 5779456 | tf_op jit(solution)/shard_map/dot_general | solution.py:246
  230.1 4.3 %collective-permute-done.24.refs_3_ = bf16[512,2176]{1,0:T(8,128)(2,1)S(1)} collective-permute-done((bf16[512,2176]{1,0:T(8,128)(2,1)S(1)}, bf16[512,2176]{1,0:T(8,128)(2,1)S(1)}, u32[]{:S(2)}, u32[]{:S(2)}) %collective-permute-start.24) | collective-permute-done | bytes 2228256 | tf_op jit(solution)/shard_map/ppermute | solution.py:299
  234.4 3.8 %row_blocks.3 = bf16[512,2176]{1,0:T(8,128)(2,1)} custom-call(s32[16]{0:T(128)S(1)} %fusion.36.places, bf16[1024,1536]{1,0:T(8,128)(2,1)} %convolution_convert_fusion.refs_0_, bf16[1024,512]{1,0:T(8,128)(2,1)S(1)} %convolution_convert_fusion.1.refs_1_, bf16[1024,128]{1,0:T(8,128)(2,1)S(1)} %fusion.21.refs_2_, ...), custom_call_target="tpu_custom_call" | custom-call | tf_op jit(solution)/shard_map/row_blocks/pallas_call | solution.py:93
  240.1 13.2 %collective-permute-done.25 = bf16[256,1024]{1,0:T(8,128)(2,1)S(1)} collective-permute-done((bf16[256,1024]{1,0:T(8,128)(2,1)S(1)}, bf16[256,1024]{1,0:T(8,128)(2,1)S(1)}, u32[]{:S(2)}, u32[]{:S(2)}) %collective-permute-start.25) | collective-permute-done | bytes 524320 | tf_op jit(solution)/shard_map/ppermute | solution.py:330
  258.5 11.9 %reduce-scatter.5.cloned.1.call-done = bf16[64,2176]{1,0:T(8,128)(2,1)} async-done(((bf16[512,2176]{1,0:T(8,128)(2,1)}), bf16[64,2176]{1,0:T(8,128)(2,1)}) %reduce-scatter.5.cloned.1.call-update) | async-done | bytes 278544 | tf_op jit(solution)/shard_map/reduce_scatter | solution.py:290
  (235 shorter events, 81.9 us)
Async XLA Ops:
  7.2 80.5 %all-gather.2.cloned.1.call-start = ((), (), s32[]{:S(2)}) async-start(), calls=%async_computation.2 | async-start | bytes 4718592 | tf_op jit(solution)/shard_map/all_gather | solution.py:287
  16.4 8.2 %collective-permute-start.3 = (bf16[64,2176]{1,0:T(8,128)(2,1)S(1)}, bf16[64,2176]{1,0:T(8,128)(2,1)S(1)}, u32[]{:S(2)}, u32[]{:S(2)}) collective-permute-start(bf16[64,2176]{1,0:T(8,128)(2,1)S(1)} %fusion.30.refs_0_), channel_id=1, source_target_pairs={{0,4},{2,6},{4,12},{6,14},{8,0},{10,2},{12,20},{14,22},{16,8},{18,... | collective-permute-start | bytes 835592 | tf_op jit(solution)/shard_map/ppermute | solution.py:299
  17.9 8.1 %collective-permute-start.1 = (bf16[64,2176]{1,0:T(8,128)(2,1)S(1)}, bf16[64,2176]{1,0:T(8,128)(2,1)S(1)}, u32[]{:S(2)}, u32[]{:S(2)}) collective-permute-start(bf16[64,2176]{1,0:T(8,128)(2,1)S(1)} %fusion.30.refs_0_), channel_id=1, source_target_pairs={{0,8},{2,10},{4,0},{6,2},{8,16},{10,18},{12,4},{14,6},{16,24},{18,... | collective-permute-start | bytes 835592 | tf_op jit(solution)/shard_map/ppermute | solution.py:299
  24.5 7.2 %collective-permute-start.4 = (bf16[64,2176]{1,0:T(8,128)(2,1)S(1)}, bf16[64,2176]{1,0:T(8,128)(2,1)S(1)}, u32[]{:S(2)}, u32[]{:S(2)}) collective-permute-start(bf16[64,2176]{1,0:T(8,128)(2,1)S(1)} %collective-permute-done.3.refs_7_), channel_id=1, source_target_pairs={{0,4},{2,6},{4,12},{6,14},{8,0},{10,2},{12,20},{14,22},{16,8},{18,... | collective-permute-start | bytes 835592 | tf_op jit(solution)/shard_map/ppermute | solution.py:299
  26.0 6.9 %collective-permute-start.2 = (bf16[64,2176]{1,0:T(8,128)(2,1)S(1)}, bf16[64,2176]{1,0:T(8,128)(2,1)S(1)}, u32[]{:S(2)}, u32[]{:S(2)}) collective-permute-start(bf16[64,2176]{1,0:T(8,128)(2,1)S(1)} %collective-permute-done.1.refs_1_), channel_id=1, source_target_pairs={{0,8},{2,10},{4,0},{6,2},{8,16},{10,18},{12,4},{14,6},{16,24},{18,... | collective-permute-start | bytes 835592 | tf_op jit(solution)/shard_map/ppermute | solution.py:299
  33.0 205.2 %reduce-scatter.3.cloned.1.call-start = ((), (), s32[]{:S(2)}) async-start(), calls=%async_computation.3 | async-start | bytes 4718592 | tf_op jit(solution)/shard_map/reduce_scatter | solution.py:290
  33.0 12.8 %collective-permute-start.5 = (bf16[256,1024]{1,0:T(8,128)(2,1)S(1)}, bf16[256,1024]{1,0:T(8,128)(2,1)S(1)}, u32[]{:S(2)}, u32[]{:S(2)}) collective-permute-start(bf16[256,1024]{1,0:T(8,128)(2,1)S(1)} %copy-done.21), channel_id=1, source_target_pairs={{0,1},{1,0},{2,3},{3,2},{4,5},{5,4},{6,7},{7,6},{8,9},{9,8},{10,11... | collective-permute-start | bytes 1572872 | tf_op jit(solution)/shard_map/ppermute | solution.py:330
  33.6 7.4 %collective-permute-start.8 = (bf16[64,2176]{1,0:T(8,128)(2,1)S(1)}, bf16[64,2176]{1,0:T(8,128)(2,1)S(1)}, u32[]{:S(2)}, u32[]{:S(2)}) collective-permute-start(bf16[64,2176]{1,0:T(8,128)(2,1)S(1)} %collective-permute-done.4.refs_6_), channel_id=1, source_target_pairs={{0,4},{2,6},{4,12},{6,14},{8,0},{10,2},{12,20},{14,22},{16,8},{18,... | collective-permute-start | bytes 835592 | tf_op jit(solution)/shard_map/ppermute | solution.py:299
  35.2 9.0 %collective-permute-start.6 = (bf16[64,2176]{1,0:T(8,128)(2,1)S(1)}, bf16[64,2176]{1,0:T(8,128)(2,1)S(1)}, u32[]{:S(2)}, u32[]{:S(2)}) collective-permute-start(bf16[64,2176]{1,0:T(8,128)(2,1)S(1)} %collective-permute-done.2.refs_2_), channel_id=1, source_target_pairs={{0,8},{2,10},{4,0},{6,2},{8,16},{10,18},{12,4},{14,6},{16,24},{18,... | collective-permute-start | bytes 835592 | tf_op jit(solution)/shard_map/ppermute | solution.py:299
  36.5 12.3 %collective-permute-start.9 = (bf16[64,2176]{1,0:T(8,128)(2,1)S(1)}, bf16[64,2176]{1,0:T(8,128)(2,1)S(1)}, u32[]{:S(2)}, u32[]{:S(2)}) collective-permute-start(bf16[64,2176]{1,0:T(8,128)(2,1)S(1)} %fusion.30.refs_0_), channel_id=1, source_target_pairs={{0,2},{2,0},{4,6},{6,4},{8,10},{10,8},{12,14},{14,12},{16,18},{18,... | collective-permute-start | bytes 835592 | tf_op jit(solution)/shard_map/ppermute | solution.py:299
  36.5 12.4 %collective-permute-start.16 = (bf16[64,2176]{1,0:T(8,128)(2,1)S(1)}, bf16[64,2176]{1,0:T(8,128)(2,1)S(1)}, u32[]{:S(2)}, u32[]{:S(2)}) collective-permute-start(bf16[64,2176]{1,0:T(8,128)(2,1)S(1)} %collective-permute-done.3.refs_7_), channel_id=1, source_target_pairs={{0,2},{2,0},{4,6},{6,4},{8,10},{10,8},{12,14},{14,12},{16,18},{18,... | collective-permute-start | bytes 835592 | tf_op jit(solution)/shard_map/ppermute | solution.py:299
  41.0 8.3 %collective-permute-start.10 = (bf16[64,2176]{1,0:T(8,128)(2,1)S(1)}, bf16[64,2176]{1,0:T(8,128)(2,1)S(1)}, u32[]{:S(2)}, u32[]{:S(2)}) collective-permute-start(bf16[64,2176]{1,0:T(8,128)(2,1)S(1)} %collective-permute-done.1.refs_1_), channel_id=1, source_target_pairs={{0,2},{2,0},{4,6},{6,4},{8,10},{10,8},{12,14},{14,12},{16,18},{18,... | collective-permute-start | bytes 835592 | tf_op jit(solution)/shard_map/ppermute | solution.py:299
  44.2 16.7 %collective-permute-start.17 = (bf16[256,1024]{1,0:T(8,128)(2,1)}, bf16[256,1024]{1,0:T(8,128)(2,1)S(1)}, u32[]{:S(2)}, u32[]{:S(2)}) collective-permute-start(bf16[256,1024]{1,0:T(8,128)(2,1)} %param.27), channel_id=1, source_target_pairs={{0,1},{1,0},{2,3},{3,2},{4,5},{5,4},{6,7},{7,6},{8,9},{9,8},{10,11... | collective-permute-start | bytes 1572872 | tf_op jit(solution)/shard_map/ppermute | solution.py:330
  46.6 14.3 %collective-permute-start.7 = (bf16[64,2176]{1,0:T(8,128)(2,1)S(1)}, bf16[64,2176]{1,0:T(8,128)(2,1)S(1)}, u32[]{:S(2)}, u32[]{:S(2)}) collective-permute-start(bf16[64,2176]{1,0:T(8,128)(2,1)S(1)} %collective-permute-done.6.refs_3_), channel_id=1, source_target_pairs={{0,8},{2,10},{4,0},{6,2},{8,16},{10,18},{12,4},{14,6},{16,24},{18,... | collective-permute-start | bytes 835592 | tf_op jit(solution)/shard_map/ppermute | solution.py:299
  48.8 13.8 %collective-permute-start.15 = (bf16[64,2176]{1,0:T(8,128)(2,1)S(1)}, bf16[64,2176]{1,0:T(8,128)(2,1)S(1)}, u32[]{:S(2)}, u32[]{:S(2)}) collective-permute-start(bf16[64,2176]{1,0:T(8,128)(2,1)S(1)} %collective-permute-done.4.refs_6_), channel_id=1, source_target_pairs={{0,2},{2,0},{4,6},{6,4},{8,10},{10,8},{12,14},{14,12},{16,18},{18,... | collective-permute-start | bytes 835592 | tf_op jit(solution)/shard_map/ppermute | solution.py:299
  48.9 13.7 %collective-permute-start.11 = (bf16[64,2176]{1,0:T(8,128)(2,1)S(1)}, bf16[64,2176]{1,0:T(8,128)(2,1)S(1)}, u32[]{:S(2)}, u32[]{:S(2)}) collective-permute-start(bf16[64,2176]{1,0:T(8,128)(2,1)S(1)} %collective-permute-done.2.refs_2_), channel_id=1, source_target_pairs={{0,2},{2,0},{4,6},{6,4},{8,10},{10,8},{12,14},{14,12},{16,18},{18,... | collective-permute-start | bytes 835592 | tf_op jit(solution)/shard_map/ppermute | solution.py:299
  49.4 13.2 %collective-permute-start.14 = (bf16[64,2176]{1,0:T(8,128)(2,1)S(1)}, bf16[64,2176]{1,0:T(8,128)(2,1)S(1)}, u32[]{:S(2)}, u32[]{:S(2)}) collective-permute-start(bf16[64,2176]{1,0:T(8,128)(2,1)S(1)} %collective-permute-done.8.refs_5_), channel_id=1, source_target_pairs={{0,2},{2,0},{4,6},{6,4},{8,10},{10,8},{12,14},{14,12},{16,18},{18,... | collective-permute-start | bytes 835592 | tf_op jit(solution)/shard_map/ppermute | solution.py:299
  87.7 29.7 %collective-permute-start.19 = (bf16[512,4096]{1,0:T(8,128)(2,1)}, bf16[512,4096]{1,0:T(8,128)(2,1)}, u32[]{:S(2)}, u32[]{:S(2)}) collective-permute-start(bf16[512,4096]{1,0:T(8,128)(2,1)} %all-gather.2.cloned.1.call-done.refs_0_), channel_id=1, source_target_pairs={{0,2},{2,0},{4,6},{6,4},{8,10},{10,8},{12,14},{14,12},{16,18},{18,... | collective-permute-start | bytes 12582920 | tf_op jit(solution)/shard_map/ppermute | solution.py:299
  87.7 25.8 %collective-permute-start.18 = (bf16[512,1024]{1,0:T(8,128)(2,1)}, bf16[512,1024]{1,0:T(8,128)(2,1)}, u32[]{:S(2)}, u32[]{:S(2)}) collective-permute-start(bf16[512,1024]{1,0:T(8,128)(2,1)} %convolution_convert_fusion.2), channel_id=1, source_target_pairs={{0,1},{1,0},{2,3},{3,2},{4,5},{5,4},{6,7},{7,6},{8,9},{9,8},{10,11... | collective-permute-start | bytes 3145736 | tf_op jit(solution)/shard_map/ppermute | solution.py:330
  146.0 7.4 %collective-permute-start.21 = (bf16[512,4096]{1,0:T(8,128)(2,1)}, bf16[512,4096]{1,0:T(8,128)(2,1)S(1)}, u32[]{:S(2)}, u32[]{:S(2)}) collective-permute-start(bf16[512,4096]{1,0:T(8,128)(2,1)} %get-tuple-element.44), channel_id=1, source_target_pairs={{0,2},{2,0},{4,6},{6,4},{8,10},{10,8},{12,14},{14,12},{16,18},{18,... | collective-permute-start | bytes 12582920 | tf_op jit(solution)/shard_map/ppermute | solution.py:299
  158.8 111.6 %reduce-scatter.5.cloned.1.call-start = ((), (), s32[]{:S(2)}) async-start(), calls=%async_computation.4 | async-start | bytes 2506752 | tf_op jit(solution)/shard_map/reduce_scatter | solution.py:290
  165.9 26.3 %collective-permute-start.20 = (bf16[512,1024]{1,0:T(8,128)(2,1)}, bf16[512,1024]{1,0:T(8,128)(2,1)}, u32[]{:S(2)}, u32[]{:S(2)}) collective-permute-start(bf16[512,1024]{1,0:T(8,128)(2,1)} %get-tuple-element.141), channel_id=1, source_target_pairs={{0,1},{1,0},{2,3},{3,2},{4,5},{5,4},{6,7},{7,6},{8,9},{9,8},{10,11... | collective-permute-start | bytes 3145736 | tf_op jit(solution)/shard_map/ppermute | solution.py:330
  173.3 38.1 %collective-permute-start.22 = (bf16[256,1024]{1,0:T(8,128)(2,1)S(1)}, bf16[256,1024]{1,0:T(8,128)(2,1)S(1)}, u32[]{:S(2)}, u32[]{:S(2)}) collective-permute-start(bf16[256,1024]{1,0:T(8,128)(2,1)S(1)} %constant_dynamic-slice_fusion.2), channel_id=1, source_target_pairs={{0,1},{1,0},{2,3},{3,2},{4,5},{5,4},{6,7},{7,6},{8,9},{9,8},{10,11... | collective-permute-start | bytes 1572872 | tf_op jit(solution)/shard_map/ppermute | solution.py:330
  239.3 14.0 %collective-permute-start.25 = (bf16[256,1024]{1,0:T(8,128)(2,1)S(1)}, bf16[256,1024]{1,0:T(8,128)(2,1)S(1)}, u32[]{:S(2)}, u32[]{:S(2)}) collective-permute-start(bf16[256,1024]{1,0:T(8,128)(2,1)S(1)} %constant_dynamic-slice_fusion.1), channel_id=1, source_target_pairs={{0,1},{1,0},{2,3},{3,2},{4,5},{5,4},{6,7},{7,6},{8,9},{9,8},{10,11... | collective-permute-start | bytes 1572872 | tf_op jit(solution)/shard_map/ppermute | solution.py:330
  (43 other events, 298.3 us)
Sparse Core Ops, SparseCore 0:
  33.1 54.5 all-gather.1
  158.9 47.7 reduce-scatter.2
  238.3 32.0 reduce-scatter.4

commit v2 on v1

--- a/solution.py
+++ b/solution.py
@@ -467,18 +467,19 @@
         g_pre = dot(grad_all, down_t, ((1,), (0,))) * slope
         g_hidden_add = jnp.sum(g_pre, axis=0)
         g_pre_b = g_pre.astype(BF16)
+        g_two_part = dot(g_pre_b, up_full, ((1,), (1,)))
+        g_two_rounded = g_two_part.astype(BF16)
+        g_norm_two = pair.total(g_two_rounded)
+        g_pre_b, act_rows, _ = tie(g_pre_b, act_rows, g_two_rounded)
         hidden_own, hidden_away = paired_products(
             along, [grad_all, in_two], [act_rows, g_pre_b], m
         )
-        g_pre_b, act_rows, hidden_away = tie(g_pre_b, act_rows, hidden_away)
-        g_two_part = dot(g_pre_b, up_full, ((1,), (1,)))
-        g_norm_two = pair.total(g_two_part)
         hidden_own = hidden_own.astype(F32) + ring.hop(hidden_away, core=1).astype(F32)
         hidden_own = hidden_own.astype(BF16)
-        g_hidden_own = ring.scatter(hidden_own)
         mlp_part = dot(act_rows, down_t, ((1,), (1,)))
         mlp_part = mlp_part.astype(BF16)
-        g_norm_two, _, _ = tie(g_norm_two, mlp_part, hidden_own)
+        g_norm_two, mlp_part, hidden_own = tie(g_norm_two, mlp_part, hidden_own)
+        g_hidden_own = ring.scatter(hidden_own)
 
         grad_rows = grad_all.astype(F32)
         g_resid = grad_rows + normalize_back(g_norm_two, normed_two, inverse_two, gains_all[1])

time: 285 us -> 291 us (1.021)
  matrix products: 44.4 us -> 40.2 us
  waiting for transfers between devices: 114 us -> 118 us
  other arithmetic: 29 us -> 32 us
    ppermute x8, waiting for transfers between devices: 55.7 us -> 67.3 us  [swap(): return lax.ppermute(value, 'tensor', [(0, 1), (1, 0)])]
    ppermute x18, waiting for transfers between devices: 41.1 us -> 33.7 us  [hop(): return lax.ppermute(value, 'fsdp', pairs)]
    dot_general x13, matrix products: 44.4 us -> 40.2 us  [dot(): lax.dot_general(left, right, (dims, ((), ())), preferred_element_type=F32)]
    reduce_sum x1, other arithmetic: 0.93 us -> 3.87 us  [shards(): jnp.sum(g_two_part * normed_two, axis=0)]
    unnamed x84 -> x88, local copies, waits for them, and re-layouts: 11 us -> 12.3 us
  transfers between devices with their start and end apart: 29 -> 29, of which waited for: 14 -> 14; matrix products, arithmetic and copies ran while one was open for 22% -> 20% of each run, Pallas kernels for 9% -> 8%
where the time goes in v2:
time: 291 us; the launch traced here: 290 us
  waiting for transfers between devices  118 us (41%)
  Pallas kernels  40.8 us (14%)
  matrix products  40.2 us (14%)
  other arithmetic  32 us (11%)
  local copies, waits for them, and re-layouts  23.8 us (8%)
  starting transfers between devices  20.1 us (7%)
  between operations  14.5 us (5%)
    ppermute x8, waiting for transfers between devices, swap(): return lax.ppermute(value, 'tensor', [(0, 1), (1, 0)])  67.3 us
    dot_general x13, matrix products, dot(): lax.dot_general(left, right, (dims, ((), ())), preferred_element_type=F32)  40.2 us
    ppermute x18, waiting for transfers between devices, hop(): return lax.ppermute(value, 'fsdp', pairs)  33.7 us
    unnamed x88, local copies, waits for them, and re-layouts  12.3 us
    ppermute x8, starting transfers between devices, swap(): return lax.ppermute(value, 'tensor', [(0, 1), (1, 0)])  11.8 us
    reduce_scatter x2, waiting for transfers between devices, scatter(): lax.psum_scatter(own, 'fsdp', scatter_dimension=0, tiled=True, axis_index...  11.5 us
    pallas_call x1, Pallas kernels, paired_products(): pl.pallas_call(multiply, grid=(2 * half,), in_specs=[pl.BlockSpec(memory_...  10.3 us
    pallas_call x1, Pallas kernels, attend_back(): pl.pallas_call(backward, grid=(seq_count, width // step), in_specs=[pl.Bl...  9.67 us
  transfers between devices with their start and end apart: 29, of which 14 were waited for; matrix products, arithmetic and copies ran while one was open for 20% of the time, Pallas kernels for 8%

profile of v2, /device:TPU:0, one launch (start us, length us, event | category | flops | bytes accessed | tf_op | source)
XLA Modules:
  0.0 289.6 jit_solution(3914645621186158054)
XLA Ops:
  18.4 6.1 %collective-permute-done.3.refs_7_ = bf16[64,2176]{1,0:T(8,128)(2,1)S(1)} collective-permute-done((bf16[64,2176]{1,0:T(8,128)(2,1)S(1)}, bf16[64,2176]{1,0:T(8,128)(2,1)S(1)}, u32[]{:S(2)}, u32[]{:S(2)}) %collective-permute-start.3) | collective-permute-done | bytes 278560 | tf_op jit(solution)/shard_map/ppermute | solution.py:299
  37.0 4.0 %collective-permute-done.8.refs_5_ = bf16[64,2176]{1,0:T(8,128)(2,1)S(1)} collective-permute-done((bf16[64,2176]{1,0:T(8,128)(2,1)S(1)}, bf16[64,2176]{1,0:T(8,128)(2,1)S(1)}, u32[]{:S(2)}, u32[]{:S(2)}) %collective-permute-start.8) | collective-permute-done | bytes 278560 | tf_op jit(solution)/shard_map/ppermute | solution.py:299
  49.5 11.4 %collective-permute-done.7.refs_4_ = bf16[64,2176]{1,0:T(8,128)(2,1)S(1)} collective-permute-done((bf16[64,2176]{1,0:T(8,128)(2,1)S(1)}, bf16[64,2176]{1,0:T(8,128)(2,1)S(1)}, u32[]{:S(2)}, u32[]{:S(2)}) %collective-permute-start.7) | collective-permute-done | bytes 278560 | tf_op jit(solution)/shard_map/ppermute | solution.py:299
  68.5 4.2 %fusion.10 = f32[512,1536]{1,0:T(8,128)S(1)} fusion(bf16[1024,2176]{1,0:T(8,128)(2,1)} %assemble.2, f32[1024]{0:T(1024)S(1)} %bitcast.107, f32[1024]{0:T(1024)S(1)} %bitcast.92, f32[512]{0:T(512)S(1)} %add_rsqrt_fusion.1, f32[512]{0:T(512)S(1)} %broadcast_multiply_fusion.3, bf16[256,1024]{1,0:T(8,128)(2,1)} %copy-done.18, bf16[256,1024]{1,0:T(8,128)(2,1)} %copy-done.16), kind=kOutput, calls=%fused_computation.19 | convolution fusion | flops 1615331328 | bytes 7352320 | tf_op jit(solution)/shard_map/dot_general | solution.py:246
  73.0 5.9 %attend.1 = bf16[512,512]{1,0:T(8,128)(2,1)S(1)} custom-call(s32[512,1]{1,0:T(8,128)S(1)} %copy.100.column, s32[1,1,512]{2,1,0:T(1,128)S(1)} %bitcast.71, bf16[512,512]{1,0:T(8,128)(2,1)S(1)} %get-tuple-element.37.query, bf16[512,512]{1,0:T(8,128)(2,1)S(1)} %slice.199.key, bf16[512,512]{1,0:T(8,128)(2,1)S(1)} %get-tuple-element.115.value), custom_call_target="tpu_custom_call" | custom-call | tf_op jit(solution)/shard_map/attend/pallas_call | solution.py:171
  82.0 5.7 %all-gather.2.cloned.1.call-done.refs_0_ = bf16[512,4096]{1,0:T(8,128)(2,1)} async-done(((bf16[64,4096]{1,0:T(8,128)(2,1)}), bf16[512,4096]{1,0:T(8,128)(2,1)}) %all-gather.2.cloned.1.call-update) | async-done | bytes 4194320 | tf_op jit(solution)/shard_map/all_gather | solution.py:287
  89.5 24.0 %collective-permute-done.18 = bf16[512,1024]{1,0:T(8,128)(2,1)} collective-permute-done((bf16[512,1024]{1,0:T(8,128)(2,1)}, bf16[512,1024]{1,0:T(8,128)(2,1)}, u32[]{:S(2)}, u32[]{:S(2)}) %collective-permute-start.18) | collective-permute-done | bytes 1048608 | tf_op jit(solution)/shard_map/ppermute | solution.py:330
  118.9 6.0 %assemble.3 = bf16[1024,4096]{1,0:T(8,128)(2,1)} custom-call(s32[16]{0:T(128)S(1)} %fusion.36.places, bf16[512,4096]{1,0:T(8,128)(2,1)S(1)} %copy-done, bf16[512,4096]{1,0:T(8,128)(2,1)} %collective-permute-done.19.refs_1_), custom_call_target="tpu_custom_call" | custom-call | tf_op jit(solution)/shard_map/assemble/pallas_call | solution.py:66
  124.9 5.3 %multiply_convert_fusion = (bf16[512,2048]{1,0:T(8,128)(2,1)S(1)}, f32[512,2048]{1,0:T(8,128)S(1)}) fusion(f32[2048]{0:T(1024)S(1)} %add.188, bf16[512,1024]{1,0:T(8,128)(2,1)S(1)} %add_convert_fusion.1.left_b, bf16[1024,4096]{1,0:T(8,128)(2,1)} %assemble.3), kind=kOutput, calls=%fused_computation.1 | convolution fusion | flops 2157969408 | bytes 11542528 | tf_op jit(solution)/shard_map/dot_general | solution.py:246
  130.2 4.6 %fusion.42 = (bf16[2048]{0:T(1024)(128)(2,1)S(1)}, bf16[512,2048]{1,0:T(8,128)(2,1)S(1)}) fusion(f32[512,2048]{1,0:T(8,128)S(1)} %get-tuple-element.144, f32[2048]{0:T(1024)S(1)} %add.188, bf16[512,1024]{1,0:T(8,128)(2,1)S(1)} %pad_maximum_fusion.1.left_a, bf16[1024,4096]{1,0:T(8,128)(2,1)S(1)} %copy-done.15), kind=kOutput, calls=%fused_computation.112 | convolution fusion | flops 2168453120 | bytes 11546624 | tf_op jit(solution)/shard_map/dot_general | solution.py:246
  134.9 3.7 %fusion.46 = (bf16[512,1024]{1,0:T(8,128)(2,1)S(1)}, f32[512,1024]{1,0:T(8,128)}) fusion(bf16[512,2048]{1,0:T(8,128)(2,1)S(1)} %get-tuple-element.42.right_b, bf16[1024,4096]{1,0:T(8,128)(2,1)S(1)} %copy-done.15), kind=kOutput, calls=%fused_computation.116 | convolution fusion | flops 2148007936 | bytes 9437184 | tf_op jit(solution)/shard_map/dot_general | solution.py:246
  138.6 10.3 %paired_products.1 = (bf16[512,4096]{1,0:T(8,128)(2,1)}, bf16[512,4096]{1,0:T(8,128)(2,1)}) custom-call(s32[16]{0:T(128)S(1)} %fusion.36.places, bf16[512,1024]{1,0:T(8,128)(2,1)S(1)} %pad_maximum_fusion.1.left_a, bf16[512,1024]{1,0:T(8,128)(2,1)S(1)} %add_convert_fusion.1.left_b, bf16[512,2048]{1,0:T(8,128)(2,1)S(1)} %get-tuple-element.41.right_a, ...), custom_call_target="tpu_custom_call" | custom-call | tf_op jit(solution)/shard_map/paired_products/pallas_call | solution.py:128
  150.4 3.4 %fusion.18 = bf16[512,1024]{1,0:T(8,128)(2,1)} fusion(bf16[512,2048]{1,0:T(8,128)(2,1)S(1)} %get-tuple-element.41.right_a, bf16[1024,4096]{1,0:T(8,128)(2,1)S(1)} %copy-done.15), kind=kOutput, calls=%fused_computation.37 | convolution fusion | flops 2148007936 | bytes 7340032 | tf_op jit(solution)/shard_map/dot_general | solution.py:246
  153.7 20.7 %collective-permute-done.20 = bf16[512,1024]{1,0:T(8,128)(2,1)S(1)} collective-permute-done((bf16[512,1024]{1,0:T(8,128)(2,1)S(1)}, bf16[512,1024]{1,0:T(8,128)(2,1)S(1)}, u32[]{:S(2)}, u32[]{:S(2)}) %collective-permute-start.20) | collective-permute-done | bytes 1048608 | tf_op jit(solution)/shard_map/ppermute | solution.py:330
  176.2 5.5 %add_convert_fusion = bf16[512,4096]{1,0:T(8,128)(2,1)} fusion(bf16[512,4096]{1,0:T(8,128)(2,1)} %collective-permute-done.21, bf16[512,4096]{1,0:T(8,128)(2,1)S(1)} %copy-done.20), kind=kLoop, calls=%fused_computation | loop fusion | flops 8388608 | bytes 12582912 | tf_op jit(solution)/shard_map/convert_element_type | solution.py:478
  182.3 3.9 %multiply_reduce_fusion = (f32[1024]{0:T(1024)S(1)}, f32[512]{0:T(512)S(1)}, f32[512]{0:T(512)S(1)}, f32[1024]{0:T(1024)S(1)}) fusion(f32[512,1024]{1,0:T(8,128)} %get-tuple-element.142, f32[512,1024]{1,0:T(8,128)} %copy-done.8, f32[512]{0:T(512)S(1)} %add_rsqrt_fusion, f32[512]{0:T(512)S(1)} %broadcast_multiply_fusion.2, f32[512,1024]{1,0:T(8,128)} %convert_add_fusion.1, ...), kind=kLoop, calls=%fused_computation.25 | loop fusion | flops 4715520 | bytes 6311936 | tf_op jit(solution)/shard_map/reduce_sum | solution.py:502
  190.4 9.7 %attend_back.1 = (bf16[512,512]{1,0:T(8,128)(2,1)S(1)}, bf16[512,512]{1,0:T(8,128)(2,1)S(1)}, bf16[512,512]{1,0:T(8,128)(2,1)S(1)}, f32[1,1,512]{2,1,0:T(1,128)S(1)}, f32[1,1,512]{2,1,0:T(1,128)S(1)}) custom-call(s32[512,1]{1,0:T(8,128)S(1)} %copy.100.column, s32[1,1,512]{2,1,0:T(1,128)S(1)} %bitcast.72, bf16[512,512]{1,0:T(8,128)(2,1)S(1)} %get-tuple-element.37.query, ...), custom_call_target="tpu_custom_call" | custom-call | tf_op jit(solution)/shard_map/attend_back/pallas_call | solution.py:220
  209.6 8.8 %collective-permute-done.22 = bf16[256,1024]{1,0:T(8,128)(2,1)S(1)} collective-permute-done((bf16[256,1024]{1,0:T(8,128)(2,1)S(1)}, bf16[256,1024]{1,0:T(8,128)(2,1)S(1)}, u32[]{:S(2)}, u32[]{:S(2)}) %collective-permute-start.22) | collective-permute-done | bytes 524320 | tf_op jit(solution)/shard_map/ppermute | solution.py:330
  220.7 5.7 %fusion.39 = (f32[1024]{0:T(1024)S(1)}, f32[1024]{0:T(1024)S(1)}, bf16[512,1024]{1,0:T(8,128)(2,1)S(1)}, f32[512,1024]{1,0:T(8,128)}) fusion(f32[512]{0:T(512)S(1)} %copy-done.33, f32[512]{0:T(512)S(1)} %copy-done.31, bf16[256,1024]{1,0:T(8,128)(2,1)S(1)} %copy-done.19, bf16[256,1024]{1,0:T(8,128)(2,1)S(1)} %copy-done.17, ...), kind=kOutput, calls=%fused_computation.110 | convolution fusion | flops 1615853568 | bytes 8925184 | tf_op jit(solution)/shard_map/dot_general | solution.py:246
  228.0 5.1 %convolution_convert_fusion.refs_0_ = bf16[1024,1536]{1,0:T(8,128)(2,1)} fusion(bf16[512,1536]{1,0:T(8,128)(2,1)} %copy-done.27, f32[1024]{0:T(1024)S(1)} %bitcast.108, f32[1024]{0:T(1024)S(1)} %bitcast.93, f32[512]{0:T(512)S(1)} %copy-done.33, f32[512]{0:T(512)S(1)} %copy-done.31, bf16[256,1024]{1,0:T(8,128)(2,1)S(1)} %copy-done.19, ...), kind=kOutput, calls=%fused_computation.5 | convolution fusion | flops 1616904192 | bytes 5779456 | tf_op jit(solution)/shard_map/dot_general | solution.py:246
  235.6 4.3 %collective-permute-done.24.refs_3_ = bf16[512,2176]{1,0:T(8,128)(2,1)S(1)} collective-permute-done((bf16[512,2176]{1,0:T(8,128)(2,1)S(1)}, bf16[512,2176]{1,0:T(8,128)(2,1)S(1)}, u32[]{:S(2)}, u32[]{:S(2)}) %collective-permute-start.24) | collective-permute-done | bytes 2228256 | tf_op jit(solution)/shard_map/ppermute | solution.py:299
  239.9 3.8 %row_blocks.3 = bf16[512,2176]{1,0:T(8,128)(2,1)} custom-call(s32[16]{0:T(128)S(1)} %fusion.36.places, bf16[1024,1536]{1,0:T(8,128)(2,1)} %convolution_convert_fusion.refs_0_, bf16[1024,512]{1,0:T(8,128)(2,1)S(1)} %convolution_convert_fusion.1.refs_1_, bf16[1024,128]{1,0:T(8,128)(2,1)S(1)} %fusion.21.refs_2_, ...), custom_call_target="tpu_custom_call" | custom-call | tf_op jit(solution)/shard_map/row_blocks/pallas_call | solution.py:93
  245.2 13.7 %collective-permute-done.25 = bf16[256,1024]{1,0:T(8,128)(2,1)} collective-permute-done((bf16[256,1024]{1,0:T(8,128)(2,1)}, bf16[256,1024]{1,0:T(8,128)(2,1)}, u32[]{:S(2)}, u32[]{:S(2)}) %collective-permute-start.25) | collective-permute-done | bytes 524320 | tf_op jit(solution)/shard_map/ppermute | solution.py:330
  264.4 11.5 %reduce-scatter.5.cloned.1.call-done = bf16[64,2176]{1,0:T(8,128)(2,1)} async-done(((bf16[512,2176]{1,0:T(8,128)(2,1)}), bf16[64,2176]{1,0:T(8,128)(2,1)}) %reduce-scatter.5.cloned.1.call-update) | async-done | bytes 278544 | tf_op jit(solution)/shard_map/reduce_scatter | solution.py:290
  (239 shorter events, 87.8 us)
Async XLA Ops:
  7.2 80.5 %all-gather.2.cloned.1.call-start = ((), (), s32[]{:S(2)}) async-start(), calls=%async_computation.2 | async-start | bytes 4718592 | tf_op jit(solution)/shard_map/all_gather | solution.py:287
  16.4 8.2 %collective-permute-start.3 = (bf16[64,2176]{1,0:T(8,128)(2,1)S(1)}, bf16[64,2176]{1,0:T(8,128)(2,1)S(1)}, u32[]{:S(2)}, u32[]{:S(2)}) collective-permute-start(bf16[64,2176]{1,0:T(8,128)(2,1)S(1)} %fusion.30.refs_0_), channel_id=1, source_target_pairs={{0,4},{2,6},{4,12},{6,14},{8,0},{10,2},{12,20},{14,22},{16,8},{18,... | collective-permute-start | bytes 835592 | tf_op jit(solution)/shard_map/ppermute | solution.py:299
  17.9 8.1 %collective-permute-start.1 = (bf16[64,2176]{1,0:T(8,128)(2,1)S(1)}, bf16[64,2176]{1,0:T(8,128)(2,1)S(1)}, u32[]{:S(2)}, u32[]{:S(2)}) collective-permute-start(bf16[64,2176]{1,0:T(8,128)(2,1)S(1)} %fusion.30.refs_0_), channel_id=1, source_target_pairs={{0,8},{2,10},{4,0},{6,2},{8,16},{10,18},{12,4},{14,6},{16,24},{18,... | collective-permute-start | bytes 835592 | tf_op jit(solution)/shard_map/ppermute | solution.py:299
  24.5 7.2 %collective-permute-start.4 = (bf16[64,2176]{1,0:T(8,128)(2,1)S(1)}, bf16[64,2176]{1,0:T(8,128)(2,1)S(1)}, u32[]{:S(2)}, u32[]{:S(2)}) collective-permute-start(bf16[64,2176]{1,0:T(8,128)(2,1)S(1)} %collective-permute-done.3.refs_7_), channel_id=1, source_target_pairs={{0,4},{2,6},{4,12},{6,14},{8,0},{10,2},{12,20},{14,22},{16,8},{18,... | collective-permute-start | bytes 835592 | tf_op jit(solution)/shard_map/ppermute | solution.py:299
  26.0 6.9 %collective-permute-start.2 = (bf16[64,2176]{1,0:T(8,128)(2,1)S(1)}, bf16[64,2176]{1,0:T(8,128)(2,1)S(1)}, u32[]{:S(2)}, u32[]{:S(2)}) collective-permute-start(bf16[64,2176]{1,0:T(8,128)(2,1)S(1)} %collective-permute-done.1.refs_1_), channel_id=1, source_target_pairs={{0,8},{2,10},{4,0},{6,2},{8,16},{10,18},{12,4},{14,6},{16,24},{18,... | collective-permute-start | bytes 835592 | tf_op jit(solution)/shard_map/ppermute | solution.py:299
  33.0 210.8 %reduce-scatter.3.cloned.1.call-start = ((), (), s32[]{:S(2)}) async-start(), calls=%async_computation.3 | async-start | bytes 4718592 | tf_op jit(solution)/shard_map/reduce_scatter | solution.py:290
  33.0 12.8 %collective-permute-start.5 = (bf16[256,1024]{1,0:T(8,128)(2,1)S(1)}, bf16[256,1024]{1,0:T(8,128)(2,1)S(1)}, u32[]{:S(2)}, u32[]{:S(2)}) collective-permute-start(bf16[256,1024]{1,0:T(8,128)(2,1)S(1)} %copy-done.24), channel_id=1, source_target_pairs={{0,1},{1,0},{2,3},{3,2},{4,5},{5,4},{6,7},{7,6},{8,9},{9,8},{10,11... | collective-permute-start | bytes 1572872 | tf_op jit(solution)/shard_map/ppermute | solution.py:330
  33.6 7.4 %collective-permute-start.8 = (bf16[64,2176]{1,0:T(8,128)(2,1)S(1)}, bf16[64,2176]{1,0:T(8,128)(2,1)S(1)}, u32[]{:S(2)}, u32[]{:S(2)}) collective-permute-start(bf16[64,2176]{1,0:T(8,128)(2,1)S(1)} %collective-permute-done.4.refs_6_), channel_id=1, source_target_pairs={{0,4},{2,6},{4,12},{6,14},{8,0},{10,2},{12,20},{14,22},{16,8},{18,... | collective-permute-start | bytes 835592 | tf_op jit(solution)/shard_map/ppermute | solution.py:299
  35.2 9.0 %collective-permute-start.6 = (bf16[64,2176]{1,0:T(8,128)(2,1)S(1)}, bf16[64,2176]{1,0:T(8,128)(2,1)S(1)}, u32[]{:S(2)}, u32[]{:S(2)}) collective-permute-start(bf16[64,2176]{1,0:T(8,128)(2,1)S(1)} %collective-permute-done.2.refs_2_), channel_id=1, source_target_pairs={{0,8},{2,10},{4,0},{6,2},{8,16},{10,18},{12,4},{14,6},{16,24},{18,... | collective-permute-start | bytes 835592 | tf_op jit(solution)/shard_map/ppermute | solution.py:299
  36.5 12.3 %collective-permute-start.9 = (bf16[64,2176]{1,0:T(8,128)(2,1)S(1)}, bf16[64,2176]{1,0:T(8,128)(2,1)S(1)}, u32[]{:S(2)}, u32[]{:S(2)}) collective-permute-start(bf16[64,2176]{1,0:T(8,128)(2,1)S(1)} %fusion.30.refs_0_), channel_id=1, source_target_pairs={{0,2},{2,0},{4,6},{6,4},{8,10},{10,8},{12,14},{14,12},{16,18},{18,... | collective-permute-start | bytes 835592 | tf_op jit(solution)/shard_map/ppermute | solution.py:299
  36.5 12.4 %collective-permute-start.16 = (bf16[64,2176]{1,0:T(8,128)(2,1)S(1)}, bf16[64,2176]{1,0:T(8,128)(2,1)S(1)}, u32[]{:S(2)}, u32[]{:S(2)}) collective-permute-start(bf16[64,2176]{1,0:T(8,128)(2,1)S(1)} %collective-permute-done.3.refs_7_), channel_id=1, source_target_pairs={{0,2},{2,0},{4,6},{6,4},{8,10},{10,8},{12,14},{14,12},{16,18},{18,... | collective-permute-start | bytes 835592 | tf_op jit(solution)/shard_map/ppermute | solution.py:299
  41.0 8.3 %collective-permute-start.10 = (bf16[64,2176]{1,0:T(8,128)(2,1)S(1)}, bf16[64,2176]{1,0:T(8,128)(2,1)S(1)}, u32[]{:S(2)}, u32[]{:S(2)}) collective-permute-start(bf16[64,2176]{1,0:T(8,128)(2,1)S(1)} %collective-permute-done.1.refs_1_), channel_id=1, source_target_pairs={{0,2},{2,0},{4,6},{6,4},{8,10},{10,8},{12,14},{14,12},{16,18},{18,... | collective-permute-start | bytes 835592 | tf_op jit(solution)/shard_map/ppermute | solution.py:299
  44.2 16.7 %collective-permute-start.17 = (bf16[256,1024]{1,0:T(8,128)(2,1)}, bf16[256,1024]{1,0:T(8,128)(2,1)S(1)}, u32[]{:S(2)}, u32[]{:S(2)}) collective-permute-start(bf16[256,1024]{1,0:T(8,128)(2,1)} %param.27), channel_id=1, source_target_pairs={{0,1},{1,0},{2,3},{3,2},{4,5},{5,4},{6,7},{7,6},{8,9},{9,8},{10,11... | collective-permute-start | bytes 1572872 | tf_op jit(solution)/shard_map/ppermute | solution.py:330
  46.6 14.3 %collective-permute-start.7 = (bf16[64,2176]{1,0:T(8,128)(2,1)S(1)}, bf16[64,2176]{1,0:T(8,128)(2,1)S(1)}, u32[]{:S(2)}, u32[]{:S(2)}) collective-permute-start(bf16[64,2176]{1,0:T(8,128)(2,1)S(1)} %collective-permute-done.6.refs_3_), channel_id=1, source_target_pairs={{0,8},{2,10},{4,0},{6,2},{8,16},{10,18},{12,4},{14,6},{16,24},{18,... | collective-permute-start | bytes 835592 | tf_op jit(solution)/shard_map/ppermute | solution.py:299
  48.8 13.8 %collective-permute-start.15 = (bf16[64,2176]{1,0:T(8,128)(2,1)S(1)}, bf16[64,2176]{1,0:T(8,128)(2,1)S(1)}, u32[]{:S(2)}, u32[]{:S(2)}) collective-permute-start(bf16[64,2176]{1,0:T(8,128)(2,1)S(1)} %collective-permute-done.4.refs_6_), channel_id=1, source_target_pairs={{0,2},{2,0},{4,6},{6,4},{8,10},{10,8},{12,14},{14,12},{16,18},{18,... | collective-permute-start | bytes 835592 | tf_op jit(solution)/shard_map/ppermute | solution.py:299
  48.9 13.7 %collective-permute-start.11 = (bf16[64,2176]{1,0:T(8,128)(2,1)S(1)}, bf16[64,2176]{1,0:T(8,128)(2,1)S(1)}, u32[]{:S(2)}, u32[]{:S(2)}) collective-permute-start(bf16[64,2176]{1,0:T(8,128)(2,1)S(1)} %collective-permute-done.2.refs_2_), channel_id=1, source_target_pairs={{0,2},{2,0},{4,6},{6,4},{8,10},{10,8},{12,14},{14,12},{16,18},{18,... | collective-permute-start | bytes 835592 | tf_op jit(solution)/shard_map/ppermute | solution.py:299
  49.4 13.2 %collective-permute-start.14 = (bf16[64,2176]{1,0:T(8,128)(2,1)S(1)}, bf16[64,2176]{1,0:T(8,128)(2,1)S(1)}, u32[]{:S(2)}, u32[]{:S(2)}) collective-permute-start(bf16[64,2176]{1,0:T(8,128)(2,1)S(1)} %collective-permute-done.8.refs_5_), channel_id=1, source_target_pairs={{0,2},{2,0},{4,6},{6,4},{8,10},{10,8},{12,14},{14,12},{16,18},{18,... | collective-permute-start | bytes 835592 | tf_op jit(solution)/shard_map/ppermute | solution.py:299
  87.7 29.6 %collective-permute-start.19 = (bf16[512,4096]{1,0:T(8,128)(2,1)}, bf16[512,4096]{1,0:T(8,128)(2,1)}, u32[]{:S(2)}, u32[]{:S(2)}) collective-permute-start(bf16[512,4096]{1,0:T(8,128)(2,1)} %all-gather.2.cloned.1.call-done.refs_0_), channel_id=1, source_target_pairs={{0,2},{2,0},{4,6},{6,4},{8,10},{10,8},{12,14},{14,12},{16,18},{18,... | collective-permute-start | bytes 12582920 | tf_op jit(solution)/shard_map/ppermute | solution.py:299
  87.7 25.8 %collective-permute-start.18 = (bf16[512,1024]{1,0:T(8,128)(2,1)}, bf16[512,1024]{1,0:T(8,128)(2,1)}, u32[]{:S(2)}, u32[]{:S(2)}) collective-permute-start(bf16[512,1024]{1,0:T(8,128)(2,1)} %convolution_convert_fusion.2), channel_id=1, source_target_pairs={{0,1},{1,0},{2,3},{3,2},{4,5},{5,4},{6,7},{7,6},{8,9},{9,8},{10,11... | collective-permute-start | bytes 3145736 | tf_op jit(solution)/shard_map/ppermute | solution.py:330
  148.9 27.3 %collective-permute-start.21 = (bf16[512,4096]{1,0:T(8,128)(2,1)}, bf16[512,4096]{1,0:T(8,128)(2,1)}, u32[]{:S(2)}, u32[]{:S(2)}) collective-permute-start(bf16[512,4096]{1,0:T(8,128)(2,1)} %get-tuple-element.44), channel_id=1, source_target_pairs={{0,2},{2,0},{4,6},{6,4},{8,10},{10,8},{12,14},{14,12},{16,18},{18,... | collective-permute-start | bytes 12582920 | tf_op jit(solution)/shard_map/ppermute | solution.py:299
  148.9 25.6 %collective-permute-start.20 = (bf16[512,1024]{1,0:T(8,128)(2,1)S(1)}, bf16[512,1024]{1,0:T(8,128)(2,1)S(1)}, u32[]{:S(2)}, u32[]{:S(2)}) collective-permute-start(bf16[512,1024]{1,0:T(8,128)(2,1)S(1)} %get-tuple-element.141), channel_id=1, source_target_pairs={{0,1},{1,0},{2,3},{3,2},{4,5},{5,4},{6,7},{7,6},{8,9},{9,8},{10,11... | collective-permute-start | bytes 3145736 | tf_op jit(solution)/shard_map/ppermute | solution.py:330
  181.7 94.3 %reduce-scatter.5.cloned.1.call-start = ((), (), s32[]{:S(2)}) async-start(), calls=%async_computation.4 | async-start | bytes 2506752 | tf_op jit(solution)/shard_map/reduce_scatter | solution.py:290
  204.8 13.6 %collective-permute-start.22 = (bf16[256,1024]{1,0:T(8,128)(2,1)S(1)}, bf16[256,1024]{1,0:T(8,128)(2,1)S(1)}, u32[]{:S(2)}, u32[]{:S(2)}) collective-permute-start(bf16[256,1024]{1,0:T(8,128)(2,1)S(1)} %constant_dynamic-slice_fusion.2), channel_id=1, source_target_pairs={{0,1},{1,0},{2,3},{3,2},{4,5},{5,4},{6,7},{7,6},{8,9},{9,8},{10,11... | collective-permute-start | bytes 1572872 | tf_op jit(solution)/shard_map/ppermute | solution.py:330
  244.7 14.3 %collective-permute-start.25 = (bf16[256,1024]{1,0:T(8,128)(2,1)}, bf16[256,1024]{1,0:T(8,128)(2,1)}, u32[]{:S(2)}, u32[]{:S(2)}) collective-permute-start(bf16[256,1024]{1,0:T(8,128)(2,1)} %constant_dynamic-slice_fusion.1), channel_id=1, source_target_pairs={{0,1},{1,0},{2,3},{3,2},{4,5},{5,4},{6,7},{7,6},{8,9},{9,8},{10,11... | collective-permute-start | bytes 1572872 | tf_op jit(solution)/shard_map/ppermute | solution.py:330
  (45 other events, 337.5 us)
Sparse Core Ops, SparseCore 0:
  33.1 54.5 all-gather.1
  181.8 47.7 reduce-scatter.2
  243.9 31.9 reduce-scatter.4
